TPU v7x, 32 devices: a whole 2x2x4 slice. The times are simulated.
32 devices in a mesh: rows: 4 (over y, x), pairs: 8 (over z, core).
Axes of the slice: x: 2, y: 2, z: 4, core: 2. Of those that a mesh axis runs over, the one named last changes fastest.
Arguments:
- latent: bfloat16 [8192, 3072], P('rows', 'pairs'), as said below
Outputs:
- rotated_latent: bfloat16 [8192, 3072], P('rows', 'pairs')
Inputs may be any that keep to these rules, and one draw needn't show every extreme that they name: `latent`: finite real entries.
All inputs are finite; a program needn't handle non-finite values.
Results may differ from a plain program's by a relative error of at most 0.0065.
Values may be sent and summed in bfloat16 or wider, within the bound.
No kernel may reach another device: no remote copies, remote signals or barrier semaphores. Data moves between devices by JAX's collectives and lax.ppermute only.
A program may use at most 64 MiB of HBM per device.

v0:
```python
import math

import jax
import jax.numpy as jnp
from jax import lax
from jax.sharding import PartitionSpec as P

ROUNDS = 2
NS_ITERS = 2


def passed_along(shard, axis, by):
    peers = lax.axis_size(axis)
    return lax.ppermute(shard, axis, [(i, (i + by) % peers) for i in range(peers)])


def orthogonal(norms, cross):
    half = cross.shape[0]
    corr = cross / jnp.sqrt(norms[:half, None] * norms[None, half:])
    total = jnp.sqrt(2.0 * jnp.sum(corr * corr) + 1e-12)
    scaled = corr * (8.0 / total)
    empty = jnp.zeros((half, half), jnp.float32)
    upper = jnp.concatenate([empty, scaled], axis=1)
    lower = jnp.concatenate([-scaled.T, empty], axis=1)
    ident = jnp.eye(2 * half, dtype=jnp.float32)
    current = (ident + jnp.concatenate([upper, lower], axis=0)) * (1.5 / math.sqrt(65.0))
    for _ in range(NS_ITERS):
        inner = jnp.dot(current.T, current, precision=lax.Precision.HIGHEST)
        current = 1.5 * current - 0.5 * jnp.dot(current, inner, precision=lax.Precision.HIGHEST)
    return current.astype(jnp.bfloat16)


def rotor_of(window):
    half = window.shape[1] // 2
    gram = jnp.dot(window.T, window, preferred_element_type=jnp.float32)
    gram = lax.psum(gram, "rows")
    return orthogonal(jnp.diagonal(gram), gram[:half, half:])


def local(latent):
    half = latent.shape[1] // 2
    window = latent
    for _ in range(ROUNDS):
        from_below = passed_along(window, "pairs", 1)
        from_above = passed_along(window, "pairs", -1)
        rotor = rotor_of(window)
        left_rotor = passed_along(rotor[:, :half], "pairs", 1)
        right_rotor = passed_along(rotor[:, half:], "pairs", -1)
        left_next = jnp.dot(from_below, left_rotor, preferred_element_type=jnp.float32).astype(
            jnp.bfloat16
        )
        right_next = jnp.dot(from_above, right_rotor, preferred_element_type=jnp.float32).astype(
            jnp.bfloat16
        )
        window = jnp.concatenate([left_next, right_next], axis=1)
    return window


def solution(mesh):
    return jax.shard_map(
        local,
        mesh=mesh,
        in_specs=(P("rows", "pairs"),),
        out_specs=P("rows", "pairs"),
        check_vma=False,
    )
```

profile of v0, /device:TPU:0, one launch (start us, length us, event | category | flops | bytes accessed | tf_op | source)
XLA Modules:
  0.0 162.5 jit_solution(6450090133549089609)
XLA Ops:
  6.5 3.9 %fusion.51 = f32[384,384]{1,0:T(8,128)} fusion(bf16[2048,384]{1,0:T(8,128)(2,1)} %param.1), kind=kOutput, calls=%fused_computation.75 | convolution fusion | flops 603979776 | bytes 2162688 | tf_op jit(solution)/shard_map/dot_general | solution.py:35
  10.4 0.0 all-reduce.7.cloned.1.call-update
  10.5 0.0 all-reduce.9.cloned.1.call-start
  10.5 4.6 %collective-permute-start.3 = (bf16[2048,384]{1,0:T(8,128)(2,1)S(1)}, bf16[2048,384]{1,0:T(8,128)(2,1)}, u32[]{:S(2)}, u32[]{:S(2)}) collective-permute-start(bf16[2048,384]{1,0:T(8,128)(2,1)S(1)} %copy-done.2), channel_id=1, source_target_pairs={{0,7},{1,0},{2,1},{3,2},{4,3},{5,4},{6,5},{7,6},{8,15},{9,8},{10,9... | collective-permute-start | bytes 4718600 | tf_op jit(solution)/shard_map/ppermute | solution.py:14
  15.1 0.0 collective-permute-start.1
  15.1 44.2 %all-reduce.7.cloned.1.call-done = f32[384,384]{1,0:T(8,128)} async-done(((f32[384,384]{1,0:T(8,128)}), f32[384,384]{1,0:T(8,128)}) %all-reduce.7.cloned.1.call-update) | async-done | bytes 589840 | tf_op jit(solution)/shard_map/psum | solution.py:36
  59.3 6.3 %gather_fusion = f32[384]{0:T(512)S(1)} fusion(f32[384,384]{1,0:T(8,128)} %all-reduce.7.cloned.1.call-done, s32[384]{0:T(512)S(1)} %or_reduce_fusion), kind=kCustom, calls=%fused_computation | custom fusion | bytes 6144 | tf_op jit(solution)/shard_map/jit(diagonal)/cond/branch_0_fun/gather | solution.py:37
  65.6 0.1 fusion.50
  65.7 0.7 multiply_reduce_fusion.1
  67.1 0.1 negate_bitcast_fusion.1
  67.3 0.1 copy.5
  67.4 1.3 fusion.12
  68.7 1.4 fusion.2
  70.2 1.3 fusion.52
  71.5 1.4 fusion.7
  72.9 2.6 %collective-permute-start.2 = (bf16[384,192]{0,1:T(8,128)(2,1)S(1)}, bf16[384,192]{0,1:T(8,128)(2,1)S(1)}, u32[]{:S(2)}, u32[]{:S(2)}) collective-permute-start(bf16[384,192]{0,1:T(8,128)(2,1)S(1)} %get-tuple-element.12), channel_id=1, source_target_pairs={{0,7},{1,0},{2,1},{3,2},{4,3},{5,4},{6,5},{7,6},{8,15},{9,8},{10,9... | collective-permute-start | bytes 442376 | tf_op jit(solution)/shard_map/ppermute | solution.py:14
  75.4 0.0 collective-permute-start
  75.4 2.7 %collective-permute-done.2 = bf16[384,192]{0,1:T(8,128)(2,1)S(1)} collective-permute-done((bf16[384,192]{0,1:T(8,128)(2,1)S(1)}, bf16[384,192]{0,1:T(8,128)(2,1)S(1)}, u32[]{:S(2)}, u32[]{:S(2)}) %collective-permute-start.2) | collective-permute-done | bytes 147488 | tf_op jit(solution)/shard_map/ppermute | solution.py:14
  78.1 0.0 collective-permute-done.3
  78.1 2.1 %fusion.1 = bf16[2048,192]{0,1:T(8,128)(2,1)S(1)} fusion(bf16[384,192]{0,1:T(8,128)(2,1)S(1)} %collective-permute-done.2, bf16[2048,384]{1,0:T(8,128)(2,1)} %collective-permute-done.3), kind=kOutput, calls=%fused_computation.7 | convolution fusion | flops 302383104 | bytes 2506752 | tf_op jit(solution)/shard_map/dot_general | solution.py:52
  80.3 1.5 collective-permute-done
  81.8 0.0 collective-permute-done.1
  81.8 2.1 %fusion = bf16[2048,192]{0,1:T(8,128)(2,1)S(1)} fusion(bf16[384,192]{0,1:T(8,128)(2,1)S(1)} %collective-permute-done, bf16[2048,384]{1,0:T(8,128)(2,1)} %collective-permute-done.1), kind=kOutput, calls=%fused_computation.6 | convolution fusion | flops 302383104 | bytes 2506752 | tf_op jit(solution)/shard_map/dot_general | solution.py:49
  83.9 1.8 %fusion.44 = f32[384,384]{1,0:T(8,128)} fusion(bf16[2048,192]{0,1:T(8,128)(2,1)S(1)} %fusion.1, bf16[2048,192]{0,1:T(8,128)(2,1)S(1)} %fusion), kind=kOutput, calls=%fused_computation.70 | convolution fusion | flops 607125504 | bytes 2162688 | tf_op jit(solution)/shard_map/dot_general | solution.py:35
  85.8 0.0 all-reduce.9.cloned.1.call-update
  85.8 1.2 pad_maximum_fusion
  87.0 2.2 %collective-permute-start.6 = (bf16[2048,384]{0,1:T(8,128)(2,1)}, bf16[2048,384]{0,1:T(8,128)(2,1)}, u32[]{:S(2)}, u32[]{:S(2)}) collective-permute-start(bf16[2048,384]{0,1:T(8,128)(2,1)} %pad_maximum_fusion), channel_id=1, source_target_pairs={{0,7},{1,0},{2,1},{3,2},{4,3},{5,4},{6,5},{7,6},{8,15},{9,8},{10,9... | collective-permute-start | bytes 4718600 | tf_op jit(solution)/shard_map/ppermute | solution.py:14
  89.3 0.0 collective-permute-start.4
  89.3 41.6 %all-reduce.9.cloned.1.call-done = f32[384,384]{1,0:T(8,128)} async-done(((f32[384,384]{1,0:T(8,128)}), f32[384,384]{1,0:T(8,128)}) %all-reduce.9.cloned.1.call-update) | async-done | bytes 589840 | tf_op jit(solution)/shard_map/psum | solution.py:36
  130.9 6.3 %gather_fusion.1 = f32[384]{0:T(512)S(1)} fusion(f32[384,384]{1,0:T(8,128)} %all-reduce.9.cloned.1.call-done, s32[384]{0:T(512)S(1)} %or_reduce_fusion), kind=kCustom, calls=%fused_computation.1 | custom fusion | bytes 6144 | tf_op jit(solution)/shard_map/jit(diagonal)/cond/branch_0_fun/gather | solution.py:37
  137.2 0.1 fusion.49
  137.2 0.8 multiply_reduce_fusion
  138.8 0.1 negate_bitcast_fusion
  138.9 0.1 copy.8
  139.0 1.3 fusion.9
  140.4 1.4 fusion.4
  141.8 1.3 fusion.53
  143.1 1.3 fusion.6
  144.4 2.6 %collective-permute-start.7 = (bf16[384,192]{0,1:T(8,128)(2,1)S(1)}, bf16[384,192]{0,1:T(8,128)(2,1)S(1)}, u32[]{:S(2)}, u32[]{:S(2)}) collective-permute-start(bf16[384,192]{0,1:T(8,128)(2,1)S(1)} %get-tuple-element.10), channel_id=1, source_target_pairs={{0,7},{1,0},{2,1},{3,2},{4,3},{5,4},{6,5},{7,6},{8,15},{9,8},{10,9... | collective-permute-start | bytes 442376 | tf_op jit(solution)/shard_map/ppermute | solution.py:14
  147.0 0.0 collective-permute-start.5
  147.0 2.7 %collective-permute-done.7 = bf16[384,192]{0,1:T(8,128)(2,1)S(1)} collective-permute-done((bf16[384,192]{0,1:T(8,128)(2,1)S(1)}, bf16[384,192]{0,1:T(8,128)(2,1)S(1)}, u32[]{:S(2)}, u32[]{:S(2)}) %collective-permute-start.7) | collective-permute-done | bytes 147488 | tf_op jit(solution)/shard_map/ppermute | solution.py:14
  149.7 0.0 collective-permute-done.6
  149.7 2.0 %convolution_convert_fusion = bf16[2048,192]{0,1:T(8,128)(2,1)S(1)} fusion(bf16[384,192]{0,1:T(8,128)(2,1)S(1)} %collective-permute-done.7, bf16[2048,384]{0,1:T(8,128)(2,1)} %collective-permute-done.6), kind=kOutput, calls=%fused_computation.2 | convolution fusion | flops 302383104 | bytes 2506752 | tf_op jit(solution)/shard_map/dot_general | solution.py:52
  151.7 1.7 %collective-permute-done.5 = bf16[384,192]{0,1:T(8,128)(2,1)S(1)} collective-permute-done((bf16[384,192]{0,1:T(8,128)(2,1)S(1)}, bf16[384,192]{0,1:T(8,128)(2,1)S(1)}, u32[]{:S(2)}, u32[]{:S(2)}) %collective-permute-start.5) | collective-permute-done | bytes 147488 | tf_op jit(solution)/shard_map/ppermute | solution.py:14
  153.4 0.0 collective-permute-done.4
  153.4 0.6 convolution_convert_fusion.1
  154.0 0.1 pad_maximum_fusion.1
  154.1 1.6 copy.7
  (10 shorter events, 0.1 us)
Async XLA Ops:
  6.5 4.0 %copy-start.2 = (bf16[2048,384]{1,0:T(8,128)(2,1)S(1)}, bf16[2048,384]{1,0:T(8,128)(2,1)}, u32[]{:S(2)}) copy-start(bf16[2048,384]{1,0:T(8,128)(2,1)} %param.1) | copy-start | bytes 4718596
  6.5 52.8 %all-reduce.7.cloned.1.call-start = ((), (), s32[]{:S(2)}) async-start(), calls=%async_computation | async-start | bytes 1179648 | tf_op jit(solution)/shard_map/psum | solution.py:36
  10.5 120.4 %all-reduce.9.cloned.1.call-start = ((), (), s32[]{:S(2)}) async-start(), calls=%async_computation.1 | async-start | bytes 1179648 | tf_op jit(solution)/shard_map/psum | solution.py:36
  10.5 67.6 %collective-permute-start.3 = (bf16[2048,384]{1,0:T(8,128)(2,1)S(1)}, bf16[2048,384]{1,0:T(8,128)(2,1)}, u32[]{:S(2)}, u32[]{:S(2)}) collective-permute-start(bf16[2048,384]{1,0:T(8,128)(2,1)S(1)} %copy-done.2), channel_id=1, source_target_pairs={{0,7},{1,0},{2,1},{3,2},{4,3},{5,4},{6,5},{7,6},{8,15},{9,8},{10,9... | collective-permute-start | bytes 4718600 | tf_op jit(solution)/shard_map/ppermute | solution.py:14
  15.1 66.7 %collective-permute-start.1 = (bf16[2048,384]{1,0:T(8,128)(2,1)S(1)}, bf16[2048,384]{1,0:T(8,128)(2,1)}, u32[]{:S(2)}, u32[]{:S(2)}) collective-permute-start(bf16[2048,384]{1,0:T(8,128)(2,1)S(1)} %copy-done.2), channel_id=1, source_target_pairs={{0,1},{1,2},{2,3},{3,4},{4,5},{5,6},{6,7},{7,0},{8,9},{9,10},{10,1... | collective-permute-start | bytes 4718600 | tf_op jit(solution)/shard_map/ppermute | solution.py:14
  59.3 6.3 %copy-start.1 = (f32[384,384]{1,0:T(8,128)S(1)}, f32[384,384]{1,0:T(8,128)}, u32[]{:S(2)}) copy-start(f32[384,384]{1,0:T(8,128)} %all-reduce.7.cloned.1.call-done) | copy-start | bytes 1769476
  72.9 5.3 %collective-permute-start.2 = (bf16[384,192]{0,1:T(8,128)(2,1)S(1)}, bf16[384,192]{0,1:T(8,128)(2,1)S(1)}, u32[]{:S(2)}, u32[]{:S(2)}) collective-permute-start(bf16[384,192]{0,1:T(8,128)(2,1)S(1)} %get-tuple-element.12), channel_id=1, source_target_pairs={{0,7},{1,0},{2,1},{3,2},{4,3},{5,4},{6,5},{7,6},{8,15},{9,8},{10,9... | collective-permute-start | bytes 442376 | tf_op jit(solution)/shard_map/ppermute | solution.py:14
  75.4 6.4 %collective-permute-start = (bf16[384,192]{0,1:T(8,128)(2,1)S(1)}, bf16[384,192]{0,1:T(8,128)(2,1)S(1)}, u32[]{:S(2)}, u32[]{:S(2)}) collective-permute-start(bf16[384,192]{0,1:T(8,128)(2,1)S(1)} %get-tuple-element.11), channel_id=1, source_target_pairs={{0,1},{1,2},{2,3},{3,4},{4,5},{5,6},{6,7},{7,0},{8,9},{9,10},{10,1... | collective-permute-start | bytes 442376 | tf_op jit(solution)/shard_map/ppermute | solution.py:14
  87.0 62.7 %collective-permute-start.6 = (bf16[2048,384]{0,1:T(8,128)(2,1)}, bf16[2048,384]{0,1:T(8,128)(2,1)}, u32[]{:S(2)}, u32[]{:S(2)}) collective-permute-start(bf16[2048,384]{0,1:T(8,128)(2,1)} %pad_maximum_fusion), channel_id=1, source_target_pairs={{0,7},{1,0},{2,1},{3,2},{4,3},{5,4},{6,5},{7,6},{8,15},{9,8},{10,9... | collective-permute-start | bytes 4718600 | tf_op jit(solution)/shard_map/ppermute | solution.py:14
  89.3 64.1 %collective-permute-start.4 = (bf16[2048,384]{0,1:T(8,128)(2,1)}, bf16[2048,384]{0,1:T(8,128)(2,1)S(1)}, u32[]{:S(2)}, u32[]{:S(2)}) collective-permute-start(bf16[2048,384]{0,1:T(8,128)(2,1)} %pad_maximum_fusion), channel_id=1, source_target_pairs={{0,1},{1,2},{2,3},{3,4},{4,5},{5,6},{6,7},{7,0},{8,9},{9,10},{10,1... | collective-permute-start | bytes 4718600 | tf_op jit(solution)/shard_map/ppermute | solution.py:14
  130.9 6.4 %copy-start = (f32[384,384]{1,0:T(8,128)S(1)}, f32[384,384]{1,0:T(8,128)}, u32[]{:S(2)}) copy-start(f32[384,384]{1,0:T(8,128)} %all-reduce.9.cloned.1.call-done) | copy-start | bytes 1769476
  144.4 5.3 %collective-permute-start.7 = (bf16[384,192]{0,1:T(8,128)(2,1)S(1)}, bf16[384,192]{0,1:T(8,128)(2,1)S(1)}, u32[]{:S(2)}, u32[]{:S(2)}) collective-permute-start(bf16[384,192]{0,1:T(8,128)(2,1)S(1)} %get-tuple-element.10), channel_id=1, source_target_pairs={{0,7},{1,0},{2,1},{3,2},{4,3},{5,4},{6,5},{7,6},{8,15},{9,8},{10,9... | collective-permute-start | bytes 442376 | tf_op jit(solution)/shard_map/ppermute | solution.py:14
  147.0 6.4 %collective-permute-start.5 = (bf16[384,192]{0,1:T(8,128)(2,1)S(1)}, bf16[384,192]{0,1:T(8,128)(2,1)S(1)}, u32[]{:S(2)}, u32[]{:S(2)}) collective-permute-start(bf16[384,192]{0,1:T(8,128)(2,1)S(1)} %get-tuple-element.9), channel_id=1, source_target_pairs={{0,1},{1,2},{2,3},{3,4},{4,5},{5,6},{6,7},{7,0},{8,9},{9,10},{10,1... | collective-permute-start | bytes 442376 | tf_op jit(solution)/shard_map/ppermute | solution.py:14
Sparse Core Ops, SparseCore 0:
  10.6 48.6 all-reduce.6
  85.9 44.8 all-reduce.8
where the time goes:
time: 163 us; the launch traced here: 162 us
  waiting for transfers between devices  94.4 us (58%)
  matrix products  23.3 us (14%)
  between operations  15 us (9%)
  local copies, waits for them, and re-layouts  14.6 us (9%)
  starting transfers between devices  12 us (7%)
  other arithmetic  3.22 us (2%)
    psum x2, waiting for transfers between devices, rotor_of(): gram = lax.psum(gram, 'rows')  85.8 us
    gather x2, local copies, waits for them, and re-layouts, rotor_of(): return orthogonal(jnp.diagonal(gram), gram[:half, half:])  12.5 us
    ppermute x8, starting transfers between devices, passed_along(): lax.ppermute(shard, axis, [(i, (i + by) % peers) for i in range(peers)])  11.9 us
    ppermute x8, waiting for transfers between devices, passed_along(): lax.ppermute(shard, axis, [(i, (i + by) % peers) for i in range(peers)])  8.62 us
    dot_general x2, matrix products, rotor_of(): gram = jnp.dot(window.T, window, preferred_element_type=jnp.float32)  5.76 us
    dot_general x4, matrix products, orthogonal(): jnp.dot(current, inner, precision=lax.Precision.HIGHEST)  5.51 us
    dot_general x4, matrix products, orthogonal(): inner = jnp.dot(current.T, current, precision=lax.Precision.HIGHEST)  5.23 us
    dot_general x2, matrix products, local(): jnp.dot(from_above, right_rotor, preferred_element_type=jnp.float32)  4.1 us
  transfers between devices with their start and end apart: 10, of which 6 were waited for; matrix products, arithmetic and copies ran while one was open for 19% of the time, Pallas kernels for 0%

commit v1 on v0

v1 whole, which is shorter than its diff:
```python
import functools
import math

import jax
import jax.numpy as jnp
import numpy as np
from jax import lax
from jax.experimental import pallas as pl
from jax.experimental.pallas import tpu as pltpu
from jax.sharding import PartitionSpec as P


F32, BF16 = jnp.float32, jnp.bfloat16
LANES = 128


def polar_coefficients():
    c = 1.5 / math.sqrt(65.0)
    mul, sub = np.polynomial.polynomial.polymul, np.polynomial.polynomial.polysub
    n = np.array([c * c, c * c])
    u = np.array([1.5 - 0.5 * c * c, -0.5 * c * c])
    return [float(v) for v in c * sub(1.5 * u, 0.5 * mul(n, mul(u, mul(u, u))))]


COEF = polar_coefficients()


def window(half):
    return -(-half // LANES) * LANES


def dot(a, b, contract):
    return lax.dot_general(a, b, ((contract[:1], contract[1:]), ((), ())), preferred_element_type=F32)


def low(a):
    return a.astype(BF16)


def params():
    return pltpu.CompilerParams(vmem_limit_bytes=16 << 20)


def whole(n):
    return [pl.BlockSpec(memory_space=pltpu.VMEM)] * n


def pieces(rows, n):
    return [slice(i * (rows // n), (i + 1) * (rows // n)) for i in range(n)]


def spans(*lists):
    cuts = {0}
    for blocks in lists:
        stop = 0
        for block in blocks:
            stop += block.shape[0]
            cuts.add(stop)
    cuts = sorted(cuts)
    return list(zip(cuts[:-1], cuts[1:]))


def span(blocks, start, stop):
    for block in blocks:
        if start < block.shape[0]:
            return block.at[start:stop]
        start, stop = start - block.shape[0], stop - block.shape[0]


def blocks_of(cols, sizes):
    return [jax.ShapeDtypeStruct((n, cols), BF16) for n in sizes]


def pack_window(top, bot, half):
    w = top.shape[1]
    lane = lax.broadcasted_iota(jnp.int32, top.shape, 1)
    return jnp.where(lane < half, pltpu.roll(top, half, 1), 0.0), jnp.where(lane >= w - half, bot, 0.0)


def unpack_window(packed):
    cols = packed.shape[1]
    half = cols // 2
    w = window(half)
    return jnp.concatenate([pltpu.roll(packed[:, :w], w - half, 1), packed[:, cols - w :]], axis=0)


def pack_stats(g_ref, cross, norms):
    half, _ = cross.shape
    h = half // 2
    packed_store(g_ref, slice(0, h), *pack_window(cross[:h], cross[h:], half), half)
    row = lax.broadcasted_iota(jnp.int32, (8, g_ref.shape[1]), 0)
    g_ref[h:] = low(jnp.where(row == 0, norms, 0.0))


def stats_shape(cols):
    return jax.ShapeDtypeStruct((cols // 4 + 8, cols), BF16)


def gram_kernel(n, x_hbm, g_ref, x_ref, sem):
    rows, cols = x_ref.shape
    half = cols // 2
    w = window(half)
    copies = [
        pltpu.make_async_copy(x_hbm.at[r, :], x_ref.at[r, :], sem.at[i]) for i, r in enumerate(pieces(rows, n))
    ]
    for copy in copies:
        copy.start()
    cross, norms = jnp.zeros((w, w), F32), jnp.zeros((1, cols), F32)
    for copy, r in zip(copies, pieces(rows, n)):
        copy.wait()
        x = x_ref[r, :]
        cross += dot(x[:, :w], x[:, cols - w :], (0, 0))
        xf = x.astype(F32)
        norms += jnp.sum(xf * xf, axis=0, keepdims=True)
    pack_stats(g_ref, cross[:half], norms)


def gram(x, n):
    rows, cols = x.shape
    w = window(cols // 2)
    x = pltpu.with_memory_space_constraint(x, pltpu.HBM)
    return pl.pallas_call(
        functools.partial(gram_kernel, n),
        in_specs=[pl.BlockSpec(memory_space=pltpu.HBM)],
        out_specs=whole(2),
        out_shape=[stats_shape(cols), jax.ShapeDtypeStruct((rows, cols), BF16)],
        scratch_shapes=[pltpu.SemaphoreType.DMA((n,))],
        cost_estimate=pl.CostEstimate(flops=2 * rows * w * w, bytes_accessed=2 * rows * cols, transcendentals=0),
        compiler_params=params(),
        name="gram",
    )(x)


def gram_pair_kernel(n_a, *refs):
    a_refs, b_refs, g_ref = refs[:n_a], refs[n_a:-1], refs[-1]
    cols = g_ref.shape[1]
    half = cols // 2
    w = window(half)
    pad, o = w - half, cols - w
    top, bot = jnp.zeros((w, w), F32), jnp.zeros((w, w), F32)
    norm_a, norm_b = jnp.zeros((1, cols), F32), jnp.zeros((1, cols), F32)
    for start, stop in spans(a_refs, b_refs):
        a, b = span(a_refs, start, stop)[...], span(b_refs, start, stop)[...]
        top += dot(a[:, :w], b[:, :w], (0, 0))
        bot += dot(a[:, o:], b[:, o:], (0, 0))
        af, bf = a.astype(F32), b.astype(F32)
        norm_a += jnp.sum(af * af, axis=0, keepdims=True)
        norm_b += jnp.sum(bf * bf, axis=0, keepdims=True)
    cross = pltpu.roll(top[:half], pad, 1) + bot[pad:]
    s, t = jnp.broadcast_to(norm_a, (8, cols)), jnp.broadcast_to(norm_b, (8, cols))
    left = s + jnp.concatenate([pltpu.roll(s[:, o:], half, 1), jnp.zeros((8, o), F32)], axis=1)
    right = t + jnp.concatenate([jnp.zeros((8, o), F32), pltpu.roll(t[:, :w], pad, 1)], axis=1)
    lane = lax.broadcasted_iota(jnp.int32, (8, cols), 1)
    pack_stats(g_ref, cross, jnp.where(lane < half, left, right)[:1])


def gram_pair(a, b):
    cols = a[0].shape[1]
    rows = sum(v.shape[0] for v in a)
    w = window(cols // 2)
    return pl.pallas_call(
        functools.partial(gram_pair_kernel, len(a)),
        in_specs=whole(len(a) + len(b)),
        out_specs=whole(1)[0],
        out_shape=stats_shape(cols),
        cost_estimate=pl.CostEstimate(flops=4 * rows * w * w, bytes_accessed=4 * rows * cols, transcendentals=0),
        compiler_params=params(),
        name="gram_pair",
    )(*a, *b)


def cross_of(parts):
    total = sum((p[...].astype(F32) for p in parts[1:]), parts[0][...].astype(F32))
    cols = total.shape[1]
    half = cols // 2
    w = window(half)
    pad, h = w - half, half // 2
    cross = unpack_window(total[:h])
    norms = total[h:]
    left = jnp.transpose(norms[:, :w])[:half, :1]
    corr = cross * (lax.rsqrt(left) * lax.rsqrt(norms[:1, cols - w :]))
    lane = lax.broadcasted_iota(jnp.int32, corr.shape, 1)
    corr = jnp.where(lane >= pad, corr, 0.0)
    size = jnp.sqrt(2.0 * jnp.sum(corr * corr) + 1e-12)
    return filled(corr * (8.0 / size))


def filled(x):
    half, w = x.shape
    return jnp.concatenate([x, jnp.zeros((w - half, w), F32)], axis=0) if w > half else x


def minus_constant(k, k2):
    return COEF[1] * k + COEF[2] * k2 + dot(low(k2), low(COEF[3] * k + COEF[4] * k2), (1, 0))


def eye_at(w, first, stop):
    r = lax.broadcasted_iota(jnp.int32, (w, w), 0)
    c = lax.broadcasted_iota(jnp.int32, (w, w), 1)
    return (r == c) & (r >= first) & (r < stop)


def left_columns(x, half):
    w = x.shape[1]
    xb = low(x)
    k = dot(xb, xb, (1, 1))
    delta = minus_constant(k, dot(low(k), low(k), (1, 0)))
    upper = delta + jnp.where(eye_at(w, 0, half), COEF[0], 0.0)
    lower = -(COEF[0] * jnp.transpose(x) + dot(xb, low(delta), (0, 0)))
    return low(jnp.concatenate([upper[:half], lower[w - half :]], axis=0))


def right_columns(x, half):
    w = x.shape[1]
    xb = low(x)
    k = dot(xb, xb, (0, 0))
    delta = minus_constant(k, dot(low(k), low(k), (1, 0)))
    upper = COEF[0] * x + dot(xb, low(delta), (1, 0))
    lower = delta + jnp.where(eye_at(w, w - half, w), COEF[0], 0.0)
    return low(jnp.concatenate([upper[:half], lower[w - half :]], axis=0))


def moved(q, by):
    return low(pltpu.roll(q.astype(F32), by, 1)) if by else q


def packed_store(ref, rows, top, bot, half):
    w = top.shape[1]
    o = 2 * half - w
    ref[rows, :o] = low(top[:, :o])
    if w > o:
        ref[rows, o:w] = low(top[:, o:] + bot[:, : w - o])
    ref[rows, w:] = low(bot[:, w - o :])


def rotate_into(refs, x_ref, q_top, q_bot):
    rows = sum(ref.shape[0] for ref in refs)
    half = x_ref.shape[1] // 2
    for start, stop in spans(refs):
        top = dot(x_ref[start:stop, :], q_top, (1, 0))
        bot = dot(x_ref[rows + start : rows + stop, :], q_bot, (1, 0))
        packed_store(span(refs, start, stop), slice(None), top, bot, half)


def rotor_kernel(n_parts, *refs):
    parts = refs[:n_parts]
    x_ref, s_ref, *a_refs = refs[n_parts:]
    half = s_ref.shape[0]
    s = cross_of(parts)
    left = left_columns(s, half)
    rotate_into(a_refs, x_ref, left, moved(left, s.shape[1] - half))
    s_ref[...] = s[:half]


def rotor(parts, x, sizes):
    rows, cols = x.shape
    w = window(cols // 2)
    s, *a = pl.pallas_call(
        functools.partial(rotor_kernel, len(parts)),
        in_specs=whole(len(parts) + 1),
        out_specs=whole(1 + len(sizes)),
        out_shape=[jax.ShapeDtypeStruct((cols // 2, w), F32)] + blocks_of(cols, sizes),
        cost_estimate=pl.CostEstimate(flops=2 * rows * cols * w, bytes_accessed=3 * rows * cols, transcendentals=0),
        compiler_params=params(),
        name="rotor",
    )(*parts, x)
    return s, a


def rotate_kernel(s_ref, x_ref, *b_refs):
    half = s_ref.shape[0]
    right = right_columns(filled(s_ref[...]), half)
    rotate_into(b_refs, x_ref, moved(right, half), right)


def rotate(s, x, sizes):
    rows, cols = x.shape
    w = s.shape[1]
    return pl.pallas_call(
        rotate_kernel,
        in_specs=whole(2),
        out_specs=whole(len(sizes)),
        out_shape=blocks_of(cols, sizes),
        cost_estimate=pl.CostEstimate(flops=2 * rows * cols * w, bytes_accessed=3 * rows * cols, transcendentals=0),
        compiler_params=params(),
        name="rotate",
    )(s, x)


def second_kernel(n_parts, *refs):
    parts = refs[:n_parts]
    s_ref, left_ref = refs[n_parts:]
    h, cols = s_ref.shape
    s = cross_of(parts)
    packed_store(s_ref, slice(None), *pack_window(s[:h], s[h : 2 * h], cols // 2), cols // 2)
    left_ref[...] = left_columns(s, cols // 2)


def second(parts):
    cols = parts[0].shape[1]
    w = window(cols // 2)
    return pl.pallas_call(
        functools.partial(second_kernel, len(parts)),
        in_specs=whole(len(parts)),
        out_specs=whole(2),
        out_shape=[jax.ShapeDtypeStruct((cols // 4, cols), BF16), jax.ShapeDtypeStruct((cols, w), BF16)],
        cost_estimate=pl.CostEstimate(flops=8 * w**3, bytes_accessed=4 * w * w, transcendentals=0),
        compiler_params=params(),
        name="second",
    )(*parts)


def right_kernel(s_ref, right_ref):
    s = unpack_window(s_ref[...].astype(F32))
    half, w = s.shape
    lane = lax.broadcasted_iota(jnp.int32, s.shape, 1)
    right_ref[...] = right_columns(filled(jnp.where(lane >= w - half, s, 0.0)), half)


def right_of(s):
    cols = s.shape[1]
    w = window(cols // 2)
    return pl.pallas_call(
        right_kernel,
        in_specs=whole(1),
        out_specs=whole(1)[0],
        out_shape=jax.ShapeDtypeStruct((cols, w), BF16),
        cost_estimate=pl.CostEstimate(flops=8 * w**3, bytes_accessed=4 * w * w, transcendentals=0),
        compiler_params=params(),
        name="right",
    )(s)


def pair_weight(q_ref, first):
    cols, w = q_ref.shape
    half = cols // 2
    rest = jnp.zeros((w - half, w), BF16)
    upper, lower = q_ref[:half], q_ref[half:]
    return jnp.concatenate([upper, rest, lower, rest] if first else [rest, upper, rest, lower], axis=0)


def pair_dot(a_refs, b_refs, start, stop, weight, first):
    w = weight.shape[1]
    cols = a_refs[0].shape[1]
    at = slice(0, w) if first else slice(cols - w, cols)
    a, b = span(a_refs, start, stop)[:, at], span(b_refs, start, stop)[:, at]
    return dot(jnp.concatenate([a, b], axis=1), weight, (1, 0))


def left_kernel(n_a, *refs):
    a_refs, (*b_refs, q_ref, o_ref) = refs[:n_a], refs[n_a:]
    rows = o_ref.shape[0] // 2
    for first in (True, False):
        weight = pair_weight(q_ref, first)
        for start, stop in spans(a_refs, b_refs):
            to = 0 if first else rows
            o_ref[to + start : to + stop, :] = low(pair_dot(a_refs, b_refs, start, stop, weight, first))


def left_half(a, b, q):
    rows, cols = sum(v.shape[0] for v in a), a[0].shape[1]
    w = q.shape[1]
    return pl.pallas_call(
        functools.partial(left_kernel, len(a)),
        in_specs=whole(len(a) + len(b) + 1),
        out_specs=whole(1)[0],
        out_shape=jax.ShapeDtypeStruct((2 * rows, w), BF16),
        cost_estimate=pl.CostEstimate(flops=8 * rows * w * w, bytes_accessed=6 * rows * cols, transcendentals=0),
        compiler_params=params(),
        name="left_half",
    )(*a, *b, q)


def final_kernel(n_a, n_b, *refs):
    a_refs, b_refs, (l_ref, q_ref, o_hbm, o_ref, sem) = refs[:n_a], refs[n_a : n_a + n_b], refs[n_a + n_b :]
    rows, cols = o_ref.shape[0] // 2, o_ref.shape[1]
    copies = []
    for first in (True, False):
        weight = pair_weight(q_ref, first)
        for start, stop in spans(a_refs, b_refs):
            to = slice(start, stop) if first else slice(rows + start, rows + stop)
            right = pair_dot(a_refs, b_refs, start, stop, weight, first)
            packed_store(o_ref, to, l_ref[to, :].astype(F32), right, cols // 2)
            copy = pltpu.make_async_copy(o_ref.at[to, :], o_hbm.at[to, :], sem.at[len(copies)])
            copy.start()
            copies.append(copy)
    for copy in copies:
        copy.wait()


def final(l, a, b, q):
    rows, cols = l.shape[0], a[0].shape[1]
    w = q.shape[1]
    return pl.pallas_call(
        functools.partial(final_kernel, len(a), len(b)),
        in_specs=whole(len(a) + len(b) + 2),
        out_specs=pl.BlockSpec(memory_space=pl.ANY),
        out_shape=jax.ShapeDtypeStruct((rows, cols), BF16),
        scratch_shapes=[pltpu.VMEM((rows, cols), BF16), pltpu.SemaphoreType.DMA((2 * len(spans(a, b)),))],
        cost_estimate=pl.CostEstimate(flops=4 * rows * w * w, bytes_accessed=4 * rows * cols, transcendentals=0),
        compiler_params=params(),
        name="final",
    )(*a, *b, l, q)


def shifted(x, axis, by):
    n = lax.axis_size(axis)
    return lax.ppermute(x, axis, [(i, (i + by) % n) for i in range(n)])


def row_parts(g):
    n = lax.axis_size("rows")
    if n & (n - 1) or n > 4:
        return [lax.psum(g.astype(F32), "rows")]
    return [g] + [lax.ppermute(g, "rows", [(i, i ^ k) for i in range(n)]) for k in range(1, n)]


def shares(rows, *eighths):
    return [rows * e // 8 for e in eighths]


def local(latent):
    rows = latent.shape[0] // 2
    stats, latent = gram(latent, 4)
    s, a = rotor(row_parts(stats), latent, shares(rows, 7, 1))
    a_in = [shifted(v, "pairs", 2) for v in a]
    b = rotate(s, latent, shares(rows, 5, 3))
    a_in[0], b_out = lax.optimization_barrier((a_in[0], b[0]))
    b_in = [shifted(b_out, "pairs", -2)]
    s, left = second(row_parts(gram_pair(a_in, b)))
    s_in = shifted(s, "pairs", -2)
    left, b_out = lax.optimization_barrier((left, b[1]))
    b_in.append(shifted(b_out, "pairs", -2))
    return final(left_half(a_in, b, left), a, b_in, right_of(s_in))


def solution(mesh):
    return jax.shard_map(
        local,
        mesh=mesh,
        in_specs=(P("rows", "pairs"),),
        out_specs=P("rows", "pairs"),
        check_vma=False,
    )
```

time: 163 us -> 54.8 us (0.34)
  waiting for transfers between devices: 94.4 us -> 29.2 us
  matrix products: 23.3 us -> 0 us
  between operations: 15 us -> 0.08 us
  local copies, waits for them, and re-layouts: 14.6 us -> 0 us
  Pallas kernels: 0 us -> 10.8 us
  other arithmetic: 3.22 us -> 0 us
  starting transfers between devices: 12 us -> 14.6 us
    psum x2 -> x0, waiting for transfers between devices: 85.8 us -> none  [rotor_of(): gram = lax.psum(gram, 'rows')]
    dot_general x14 -> x0, matrix products: 23.3 us -> none  [the longest x2 5.76 us: rotor_of(): gram = jnp.dot(window.T, window, preferred_element_type=jnp.float32)]
    ppermute x8 -> x11, waiting for transfers between devices: 8.62 us -> 29.2 us  [the longest x5 21.5 us: shifted(): return lax.ppermute(x, axis, [(i, (i + by) % n) for i in range(n)])]
    gather x2 -> x0, local copies, waits for them, and re-layouts: 12.5 us -> none  [rotor_of(): return orthogonal(jnp.diagonal(gram), gram[:half, half:])]
    pallas_call x0 -> x8, Pallas kernels: none -> 10.8 us  [the longest x1 2.24 us: gram(): pl.pallas_call(functools.partial(gram_kernel, n), in_specs=[pl.BlockSpec(...]
    ppermute x8 -> x11, starting transfers between devices: 11.9 us -> 14.6 us  [the longest x6 8.18 us: row_parts(): lax.ppermute(g, 'rows', [(i, i ^ k) for i in range(n)])]
  transfers between devices with their start and end apart: 10 -> 11, of which waited for: 6 -> 9; matrix products, arithmetic and copies ran while one was open for 19% -> 0% of each run, Pallas kernels for 0% -> 9%
where the time goes in v1:
time: 54.8 us; the launch traced here: 54.6 us
  waiting for transfers between devices  29.2 us (53%)
  starting transfers between devices  14.6 us (27%)
  Pallas kernels  10.8 us (20%)
    ppermute x5, waiting for transfers between devices, shifted(): return lax.ppermute(x, axis, [(i, (i + by) % n) for i in range(n)])  21.5 us
    ppermute x6, starting transfers between devices, row_parts(): lax.ppermute(g, 'rows', [(i, i ^ k) for i in range(n)])  8.18 us
    ppermute x6, waiting for transfers between devices, row_parts(): lax.ppermute(g, 'rows', [(i, i ^ k) for i in range(n)])  7.75 us
    ppermute x5, starting transfers between devices, shifted(): return lax.ppermute(x, axis, [(i, (i + by) % n) for i in range(n)])  6.38 us
    pallas_call x1, Pallas kernels, gram(): pl.pallas_call(functools.partial(gram_kernel, n), in_specs=[pl.BlockSpec(...  2.24 us
    pallas_call x1, Pallas kernels, rotor(): pl.pallas_call(functools.partial(rotor_kernel, len(parts)), in_specs=whol...  1.93 us
    pallas_call x1, Pallas kernels, final(): pl.pallas_call(functools.partial(final_kernel, len(a), len(b)), in_specs=...  1.7 us
    pallas_call x1, Pallas kernels, rotate(): pl.pallas_call(rotate_kernel, in_specs=whole(2), out_specs=whole(len(size...  1.52 us
  transfers between devices with their start and end apart: 11, of which 9 were waited for; matrix products, arithmetic and copies ran while one was open for 0% of the time, Pallas kernels for 9%

profile of v1, /device:TPU:0, one launch (start us, length us, event | category | flops | bytes accessed | tf_op | source)
XLA Modules:
  0.0 54.6 jit_solution(15259128238388114420)
XLA Ops:
  0.0 2.2 %gram.1 = (bf16[104,384]{1,0:T(8,128)(2,1)S(1)}, bf16[2048,384]{1,0:T(8,128)(2,1)S(1)}) custom-call(bf16[2048,384]{1,0:T(8,128)(2,1)} %x_hbm.1), custom_call_target="tpu_custom_call" | custom-call | flops 268435456 | bytes 1572864 | tf_op jit(solution)/shard_map/gram/pallas_call | solution.py:122
  2.2 4.0 %collective-permute-start.2 = (bf16[104,384]{1,0:T(8,128)(2,1)S(1)}, bf16[104,384]{1,0:T(8,128)(2,1)S(1)}, u32[]{:S(2)}, u32[]{:S(2)}) collective-permute-start(bf16[104,384]{1,0:T(8,128)(2,1)S(1)} %get-tuple-element.18.refs_0_), channel_id=1, source_target_pairs={{0,24},{8,16},{16,8},{24,0},{1,25},{9,17},{17,9},{25,1},{2,26},{10... | collective-permute-start | bytes 239624 | tf_op jit(solution)/shard_map/ppermute | solution.py:415
  6.2 0.5 collective-permute-start.1
  6.7 0.1 collective-permute-start
  6.9 1.9 %collective-permute-done.2.refs_3_ = bf16[104,384]{1,0:T(8,128)(2,1)S(1)} collective-permute-done((bf16[104,384]{1,0:T(8,128)(2,1)S(1)}, bf16[104,384]{1,0:T(8,128)(2,1)S(1)}, u32[]{:S(2)}, u32[]{:S(2)}) %collective-permute-start.2) | collective-permute-done | bytes 79904 | tf_op jit(solution)/shard_map/ppermute | solution.py:415
  8.7 1.9 %collective-permute-done.1.refs_2_ = bf16[104,384]{1,0:T(8,128)(2,1)S(1)} collective-permute-done((bf16[104,384]{1,0:T(8,128)(2,1)S(1)}, bf16[104,384]{1,0:T(8,128)(2,1)S(1)}, u32[]{:S(2)}, u32[]{:S(2)}) %collective-permute-start.1) | collective-permute-done | bytes 79904 | tf_op jit(solution)/shard_map/ppermute | solution.py:415
  10.7 0.5 collective-permute-done.refs_1_
  11.2 1.9 %rotor.1 = (f32[192,256]{1,0:T(8,128)S(1)}, bf16[896,384]{1,0:T(8,128)(2,1)S(1)}, bf16[128,384]{1,0:T(8,128)(2,1)S(1)}) custom-call(bf16[104,384]{1,0:T(8,128)(2,1)S(1)} %get-tuple-element.18.refs_0_, bf16[104,384]{1,0:T(8,128)(2,1)S(1)} %collective-permute-done.refs_1_, bf16[104,384]{1,0:T(8,128)(2,1)S(1)} %collective-permute-done.1.refs_2_, ...), custom_call_target="tpu_custom_call" | custom-call | flops 402653184 | bytes 2359296 | tf_op jit(solution)/shard_map/rotor/pallas_call | solution.py:258
  13.1 1.6 %collective-permute-start.3 = (bf16[896,384]{1,0:T(8,128)(2,1)S(1)}, bf16[896,384]{1,0:T(8,128)(2,1)S(1)}, u32[]{:S(2)}, u32[]{:S(2)}) collective-permute-start(bf16[896,384]{1,0:T(8,128)(2,1)S(1)} %get-tuple-element.20.refs_0_), channel_id=1, source_target_pairs={{0,2},{1,3},{2,4},{3,5},{4,6},{5,7},{6,0},{7,1},{8,10},{9,11},{10,... | collective-permute-start | bytes 2064392 | tf_op jit(solution)/shard_map/ppermute | solution.py:408
  14.7 1.6 %collective-permute-start.5 = (bf16[128,384]{1,0:T(8,128)(2,1)S(1)}, bf16[128,384]{1,0:T(8,128)(2,1)S(1)}, u32[]{:S(2)}, u32[]{:S(2)}) collective-permute-start(bf16[128,384]{1,0:T(8,128)(2,1)S(1)} %get-tuple-element.21.refs_1_), channel_id=1, source_target_pairs={{0,2},{1,3},{2,4},{3,5},{4,6},{5,7},{6,0},{7,1},{8,10},{9,11},{10,... | collective-permute-start | bytes 294920 | tf_op jit(solution)/shard_map/ppermute | solution.py:408
  16.3 1.5 %rotate.1 = (bf16[640,384]{1,0:T(8,128)(2,1)S(1)}, bf16[384,384]{1,0:T(8,128)(2,1)S(1)}) custom-call(f32[192,256]{1,0:T(8,128)S(1)} %get-tuple-element.22.s_ref, bf16[2048,384]{1,0:T(8,128)(2,1)S(1)} %get-tuple-element.19.refs_4_.x_ref), custom_call_target="tpu_custom_call" | custom-call | flops 402653184 | bytes 2359296 | tf_op jit(solution)/shard_map/rotate/pallas_call | solution.py:279
  17.8 14.8 %collective-permute-done.3.refs_0_ = bf16[896,384]{1,0:T(8,128)(2,1)S(1)} collective-permute-done((bf16[896,384]{1,0:T(8,128)(2,1)S(1)}, bf16[896,384]{1,0:T(8,128)(2,1)S(1)}, u32[]{:S(2)}, u32[]{:S(2)}) %collective-permute-start.3) | collective-permute-done | bytes 688160 | tf_op jit(solution)/shard_map/ppermute | solution.py:408
  32.6 1.6 %collective-permute-start.4 = (bf16[640,384]{1,0:T(8,128)(2,1)S(1)}, bf16[640,384]{1,0:T(8,128)(2,1)S(1)}, u32[]{:S(2)}, u32[]{:S(2)}) collective-permute-start(bf16[640,384]{1,0:T(8,128)(2,1)S(1)} %get-tuple-element.24.refs_2_), channel_id=1, source_target_pairs={{0,6},{1,7},{2,0},{3,1},{4,2},{5,3},{6,4},{7,5},{8,14},{9,15},{10,... | collective-permute-start | bytes 1474568 | tf_op jit(solution)/shard_map/ppermute | solution.py:408
  34.2 0.4 collective-permute-done.5.refs_1_
  34.7 0.6 %gram_pair.1.refs_0_ = bf16[104,384]{1,0:T(8,128)(2,1)S(1)} custom-call(bf16[896,384]{1,0:T(8,128)(2,1)S(1)} %collective-permute-done.3.refs_0_, bf16[128,384]{1,0:T(8,128)(2,1)S(1)} %collective-permute-done.5.refs_1_, bf16[640,384]{1,0:T(8,128)(2,1)S(1)} %get-tuple-element.24.refs_2_, bf16[384,384]{1,0:T(8,128)(2,1)S(1)} %get-tuple-element.28.refs_3_), custom_call_target="tpu_custom_call" | custom-call | flops 268435456 | bytes 1572864 | tf_op jit(solution)/shard_map/gram_pair/pallas_call | solution.py:161
  35.3 1.6 %collective-permute-start.8 = (bf16[104,384]{1,0:T(8,128)(2,1)S(1)}, bf16[104,384]{1,0:T(8,128)(2,1)S(1)}, u32[]{:S(2)}, u32[]{:S(2)}) collective-permute-start(bf16[104,384]{1,0:T(8,128)(2,1)S(1)} %gram_pair.1.refs_0_), channel_id=1, source_target_pairs={{0,24},{8,16},{16,8},{24,0},{1,25},{9,17},{17,9},{25,1},{2,26},{10... | collective-permute-start | bytes 239624 | tf_op jit(solution)/shard_map/ppermute | solution.py:415
  36.9 1.0 %collective-permute-start.7 = (bf16[104,384]{1,0:T(8,128)(2,1)S(1)}, bf16[104,384]{1,0:T(8,128)(2,1)S(1)}, u32[]{:S(2)}, u32[]{:S(2)}) collective-permute-start(bf16[104,384]{1,0:T(8,128)(2,1)S(1)} %gram_pair.1.refs_0_), channel_id=1, source_target_pairs={{0,16},{8,24},{16,0},{24,8},{1,17},{9,25},{17,1},{25,9},{2,18},{10... | collective-permute-start | bytes 239624 | tf_op jit(solution)/shard_map/ppermute | solution.py:415
  37.9 0.9 %collective-permute-start.6 = (bf16[104,384]{1,0:T(8,128)(2,1)S(1)}, bf16[104,384]{1,0:T(8,128)(2,1)S(1)}, u32[]{:S(2)}, u32[]{:S(2)}) collective-permute-start(bf16[104,384]{1,0:T(8,128)(2,1)S(1)} %gram_pair.1.refs_0_), channel_id=1, source_target_pairs={{0,8},{8,0},{16,24},{24,16},{1,9},{9,1},{17,25},{25,17},{2,10},{10... | collective-permute-start | bytes 239624 | tf_op jit(solution)/shard_map/ppermute | solution.py:415
  38.9 1.9 %collective-permute-done.8.refs_3_ = bf16[104,384]{1,0:T(8,128)(2,1)S(1)} collective-permute-done((bf16[104,384]{1,0:T(8,128)(2,1)S(1)}, bf16[104,384]{1,0:T(8,128)(2,1)S(1)}, u32[]{:S(2)}, u32[]{:S(2)}) %collective-permute-start.8) | collective-permute-done | bytes 79904 | tf_op jit(solution)/shard_map/ppermute | solution.py:415
  40.7 0.8 %collective-permute-done.7.refs_2_ = bf16[104,384]{1,0:T(8,128)(2,1)S(1)} collective-permute-done((bf16[104,384]{1,0:T(8,128)(2,1)S(1)}, bf16[104,384]{1,0:T(8,128)(2,1)S(1)}, u32[]{:S(2)}, u32[]{:S(2)}) %collective-permute-start.7) | collective-permute-done | bytes 79904 | tf_op jit(solution)/shard_map/ppermute | solution.py:415
  41.5 0.8 %collective-permute-done.6.refs_1_ = bf16[104,384]{1,0:T(8,128)(2,1)S(1)} collective-permute-done((bf16[104,384]{1,0:T(8,128)(2,1)S(1)}, bf16[104,384]{1,0:T(8,128)(2,1)S(1)}, u32[]{:S(2)}, u32[]{:S(2)}) %collective-permute-start.6) | collective-permute-done | bytes 79904 | tf_op jit(solution)/shard_map/ppermute | solution.py:415
  42.3 1.2 %second.1 = (bf16[96,384]{1,0:T(8,128)(2,1)S(1)}, bf16[384,256]{1,0:T(8,128)(2,1)S(1)}) custom-call(bf16[104,384]{1,0:T(8,128)(2,1)S(1)} %gram_pair.1.refs_0_, bf16[104,384]{1,0:T(8,128)(2,1)S(1)} %collective-permute-done.6.refs_1_, bf16[104,384]{1,0:T(8,128)(2,1)S(1)} %collective-permute-done.7.refs_2_, bf16[104,384]{1,0:T(8,128)(2,1)S(1)} %collective-permute-done.8.refs_3_), custom_call_target="tpu_custom_call" | custom-call | flops 134217728 | bytes 262144 | tf_op jit(solution)/shard_map/second/pallas_call | solution.py:302
  43.6 1.1 %collective-permute-start.9 = (bf16[384,384]{1,0:T(8,128)(2,1)S(1)}, bf16[384,384]{1,0:T(8,128)(2,1)S(1)}, u32[]{:S(2)}, u32[]{:S(2)}) collective-permute-start(bf16[384,384]{1,0:T(8,128)(2,1)S(1)} %get-tuple-element.28.refs_3_), channel_id=1, source_target_pairs={{0,6},{1,7},{2,0},{3,1},{4,2},{5,3},{6,4},{7,5},{8,14},{9,15},{10,... | collective-permute-start | bytes 884744 | tf_op jit(solution)/shard_map/ppermute | solution.py:408
  44.7 0.4 collective-permute-start.10
  45.1 0.7 %left_half.1.refs_4_ = bf16[2048,256]{1,0:T(8,128)(2,1)S(1)} custom-call(bf16[896,384]{1,0:T(8,128)(2,1)S(1)} %collective-permute-done.3.refs_0_, bf16[128,384]{1,0:T(8,128)(2,1)S(1)} %collective-permute-done.5.refs_1_, bf16[640,384]{1,0:T(8,128)(2,1)S(1)} %get-tuple-element.24.refs_2_, bf16[384,384]{1,0:T(8,128)(2,1)S(1)} %get-tuple-element.28.refs_3_, ...), custom_call_target="tpu_custom_call" | custom-call | flops 536870912 | bytes 2359296 | tf_op jit(solution)/shard_map/left_half/pallas_call | solution.py:363
  45.8 6.2 %collective-permute-done.10.s_ref = bf16[96,384]{1,0:T(8,128)(2,1)S(1)} collective-permute-done((bf16[96,384]{1,0:T(8,128)(2,1)S(1)}, bf16[96,384]{1,0:T(8,128)(2,1)S(1)}, u32[]{:S(2)}, u32[]{:S(2)}) %collective-permute-start.10) | collective-permute-done | bytes 73760 | tf_op jit(solution)/shard_map/ppermute | solution.py:408
  52.1 0.9 %right.1.refs_5_ = bf16[384,256]{1,0:T(8,128)(2,1)S(1)} custom-call(bf16[96,384]{1,0:T(8,128)(2,1)S(1)} %collective-permute-done.10.s_ref), custom_call_target="tpu_custom_call" | custom-call | flops 134217728 | bytes 262144 | tf_op jit(solution)/shard_map/right/pallas_call | solution.py:323
  52.9 0.0 collective-permute-done.9.refs_3_
  52.9 0.0 collective-permute-done.4.refs_2_
  52.9 1.7 %final.1 = bf16[2048,384]{1,0:T(8,128)(2,1)} custom-call(bf16[896,384]{1,0:T(8,128)(2,1)S(1)} %get-tuple-element.20.refs_0_, bf16[128,384]{1,0:T(8,128)(2,1)S(1)} %get-tuple-element.21.refs_1_, bf16[640,384]{1,0:T(8,128)(2,1)S(1)} %collective-permute-done.4.refs_2_, bf16[384,384]{1,0:T(8,128)(2,1)S(1)} %collective-permute-done.9.refs_3_, ...), custom_call_target="tpu_custom_call" | custom-call | flops 536870912 | bytes 3145728 | tf_op jit(solution)/shard_map/final/pallas_call | solution.py:394
Async XLA Ops:
  2.2 6.5 %collective-permute-start.2 = (bf16[104,384]{1,0:T(8,128)(2,1)S(1)}, bf16[104,384]{1,0:T(8,128)(2,1)S(1)}, u32[]{:S(2)}, u32[]{:S(2)}) collective-permute-start(bf16[104,384]{1,0:T(8,128)(2,1)S(1)} %get-tuple-element.18.refs_0_), channel_id=1, source_target_pairs={{0,24},{8,16},{16,8},{24,0},{1,25},{9,17},{17,9},{25,1},{2,26},{10... | collective-permute-start | bytes 239624 | tf_op jit(solution)/shard_map/ppermute | solution.py:415
  6.2 4.4 %collective-permute-start.1 = (bf16[104,384]{1,0:T(8,128)(2,1)S(1)}, bf16[104,384]{1,0:T(8,128)(2,1)S(1)}, u32[]{:S(2)}, u32[]{:S(2)}) collective-permute-start(bf16[104,384]{1,0:T(8,128)(2,1)S(1)} %get-tuple-element.18.refs_0_), channel_id=1, source_target_pairs={{0,16},{8,24},{16,0},{24,8},{1,17},{9,25},{17,1},{25,9},{2,18},{10... | collective-permute-start | bytes 239624 | tf_op jit(solution)/shard_map/ppermute | solution.py:415
  6.7 4.4 %collective-permute-start = (bf16[104,384]{1,0:T(8,128)(2,1)S(1)}, bf16[104,384]{1,0:T(8,128)(2,1)S(1)}, u32[]{:S(2)}, u32[]{:S(2)}) collective-permute-start(bf16[104,384]{1,0:T(8,128)(2,1)S(1)} %get-tuple-element.18.refs_0_), channel_id=1, source_target_pairs={{0,8},{8,0},{16,24},{24,16},{1,9},{9,1},{17,25},{25,17},{2,10},{10... | collective-permute-start | bytes 239624 | tf_op jit(solution)/shard_map/ppermute | solution.py:415
  13.1 19.5 %collective-permute-start.3 = (bf16[896,384]{1,0:T(8,128)(2,1)S(1)}, bf16[896,384]{1,0:T(8,128)(2,1)S(1)}, u32[]{:S(2)}, u32[]{:S(2)}) collective-permute-start(bf16[896,384]{1,0:T(8,128)(2,1)S(1)} %get-tuple-element.20.refs_0_), channel_id=1, source_target_pairs={{0,2},{1,3},{2,4},{3,5},{4,6},{5,7},{6,0},{7,1},{8,10},{9,11},{10,... | collective-permute-start | bytes 2064392 | tf_op jit(solution)/shard_map/ppermute | solution.py:408
  14.7 19.9 %collective-permute-start.5 = (bf16[128,384]{1,0:T(8,128)(2,1)S(1)}, bf16[128,384]{1,0:T(8,128)(2,1)S(1)}, u32[]{:S(2)}, u32[]{:S(2)}) collective-permute-start(bf16[128,384]{1,0:T(8,128)(2,1)S(1)} %get-tuple-element.21.refs_1_), channel_id=1, source_target_pairs={{0,2},{1,3},{2,4},{3,5},{4,6},{5,7},{6,0},{7,1},{8,10},{9,11},{10,... | collective-permute-start | bytes 294920 | tf_op jit(solution)/shard_map/ppermute | solution.py:408
  32.6 20.3 %collective-permute-start.4 = (bf16[640,384]{1,0:T(8,128)(2,1)S(1)}, bf16[640,384]{1,0:T(8,128)(2,1)S(1)}, u32[]{:S(2)}, u32[]{:S(2)}) collective-permute-start(bf16[640,384]{1,0:T(8,128)(2,1)S(1)} %get-tuple-element.24.refs_2_), channel_id=1, source_target_pairs={{0,6},{1,7},{2,0},{3,1},{4,2},{5,3},{6,4},{7,5},{8,14},{9,15},{10,... | collective-permute-start | bytes 1474568 | tf_op jit(solution)/shard_map/ppermute | solution.py:408
  35.3 5.4 %collective-permute-start.8 = (bf16[104,384]{1,0:T(8,128)(2,1)S(1)}, bf16[104,384]{1,0:T(8,128)(2,1)S(1)}, u32[]{:S(2)}, u32[]{:S(2)}) collective-permute-start(bf16[104,384]{1,0:T(8,128)(2,1)S(1)} %gram_pair.1.refs_0_), channel_id=1, source_target_pairs={{0,24},{8,16},{16,8},{24,0},{1,25},{9,17},{17,9},{25,1},{2,26},{10... | collective-permute-start | bytes 239624 | tf_op jit(solution)/shard_map/ppermute | solution.py:415
  36.9 4.7 %collective-permute-start.7 = (bf16[104,384]{1,0:T(8,128)(2,1)S(1)}, bf16[104,384]{1,0:T(8,128)(2,1)S(1)}, u32[]{:S(2)}, u32[]{:S(2)}) collective-permute-start(bf16[104,384]{1,0:T(8,128)(2,1)S(1)} %gram_pair.1.refs_0_), channel_id=1, source_target_pairs={{0,16},{8,24},{16,0},{24,8},{1,17},{9,25},{17,1},{25,9},{2,18},{10... | collective-permute-start | bytes 239624 | tf_op jit(solution)/shard_map/ppermute | solution.py:415
  37.9 4.4 %collective-permute-start.6 = (bf16[104,384]{1,0:T(8,128)(2,1)S(1)}, bf16[104,384]{1,0:T(8,128)(2,1)S(1)}, u32[]{:S(2)}, u32[]{:S(2)}) collective-permute-start(bf16[104,384]{1,0:T(8,128)(2,1)S(1)} %gram_pair.1.refs_0_), channel_id=1, source_target_pairs={{0,8},{8,0},{16,24},{24,16},{1,9},{9,1},{17,25},{25,17},{2,10},{10... | collective-permute-start | bytes 239624 | tf_op jit(solution)/shard_map/ppermute | solution.py:415
  43.6 9.4 %collective-permute-start.9 = (bf16[384,384]{1,0:T(8,128)(2,1)S(1)}, bf16[384,384]{1,0:T(8,128)(2,1)S(1)}, u32[]{:S(2)}, u32[]{:S(2)}) collective-permute-start(bf16[384,384]{1,0:T(8,128)(2,1)S(1)} %get-tuple-element.28.refs_3_), channel_id=1, source_target_pairs={{0,6},{1,7},{2,0},{3,1},{4,2},{5,3},{6,4},{7,5},{8,14},{9,15},{10,... | collective-permute-start | bytes 884744 | tf_op jit(solution)/shard_map/ppermute | solution.py:408
  44.7 7.4 %collective-permute-start.10 = (bf16[96,384]{1,0:T(8,128)(2,1)S(1)}, bf16[96,384]{1,0:T(8,128)(2,1)S(1)}, u32[]{:S(2)}, u32[]{:S(2)}) collective-permute-start(bf16[96,384]{1,0:T(8,128)(2,1)S(1)} %get-tuple-element.30), channel_id=1, source_target_pairs={{0,6},{1,7},{2,0},{3,1},{4,2},{5,3},{6,4},{7,5},{8,14},{9,15},{10,... | collective-permute-start | bytes 221192 | tf_op jit(solution)/shard_map/ppermute | solution.py:408

commit v2 on v1

--- a/solution.py
+++ b/solution.py
@@ -96,18 +96,38 @@
     return jax.ShapeDtypeStruct((cols // 4 + 8, cols), BF16)
 
 
-def gram_kernel(n, x_hbm, g_ref, x_ref, sem):
+def taken_kernel(x_hbm, raw_ref, sem):
+    rows, k = x_hbm.shape[0], raw_ref.shape[0] // 2
+    copies = [
+        pltpu.make_async_copy(x_hbm.at[stop - k : stop, :], raw_ref.at[i * k : (i + 1) * k, :], sem.at[i])
+        for i, stop in enumerate((rows // 2, rows))
+    ]
+    for copy in copies:
+        copy.start()
+    for copy in copies:
+        copy.wait()
+
+
+def taken(x, k):
+    cols = x.shape[1]
+    return pl.pallas_call(
+        taken_kernel,
+        in_specs=[pl.BlockSpec(memory_space=pltpu.HBM)],
+        out_specs=whole(1)[0],
+        out_shape=jax.ShapeDtypeStruct((2 * k, cols), BF16),
+        scratch_shapes=[pltpu.SemaphoreType.DMA((2,))],
+        cost_estimate=pl.CostEstimate(flops=0, bytes_accessed=8 * k * cols, transcendentals=0),
+        compiler_params=params(),
+        name="taken",
+    )(pltpu.with_memory_space_constraint(x, pltpu.HBM))
+
+
+def gram_kernel(n, x_ref, g_ref):
     rows, cols = x_ref.shape
     half = cols // 2
     w = window(half)
-    copies = [
-        pltpu.make_async_copy(x_hbm.at[r, :], x_ref.at[r, :], sem.at[i]) for i, r in enumerate(pieces(rows, n))
-    ]
-    for copy in copies:
-        copy.start()
     cross, norms = jnp.zeros((w, w), F32), jnp.zeros((1, cols), F32)
-    for copy, r in zip(copies, pieces(rows, n)):
-        copy.wait()
+    for r in pieces(rows, n):
         x = x_ref[r, :]
         cross += dot(x[:, :w], x[:, cols - w :], (0, 0))
         xf = x.astype(F32)
@@ -118,13 +138,11 @@
 def gram(x, n):
     rows, cols = x.shape
     w = window(cols // 2)
-    x = pltpu.with_memory_space_constraint(x, pltpu.HBM)
     return pl.pallas_call(
         functools.partial(gram_kernel, n),
-        in_specs=[pl.BlockSpec(memory_space=pltpu.HBM)],
-        out_specs=whole(2),
-        out_shape=[stats_shape(cols), jax.ShapeDtypeStruct((rows, cols), BF16)],
-        scratch_shapes=[pltpu.SemaphoreType.DMA((n,))],
+        in_specs=whole(1),
+        out_specs=whole(1)[0],
+        out_shape=stats_shape(cols),
         cost_estimate=pl.CostEstimate(flops=2 * rows * w * w, bytes_accessed=2 * rows * cols, transcendentals=0),
         compiler_params=params(),
         name="gram",
@@ -233,49 +251,81 @@
     ref[rows, w:] = low(bot[:, w - o :])
 
 
-def rotate_into(refs, x_ref, q_top, q_bot):
-    rows = sum(ref.shape[0] for ref in refs)
-    half = x_ref.shape[1] // 2
+def rotate_into(refs, x_ref, q_top, q_bot, base=0):
+    rows, half = x_ref.shape[0] // 2, x_ref.shape[1] // 2
     for start, stop in spans(refs):
-        top = dot(x_ref[start:stop, :], q_top, (1, 0))
-        bot = dot(x_ref[rows + start : rows + stop, :], q_bot, (1, 0))
+        top = dot(x_ref[base + start : base + stop, :], q_top, (1, 0))
+        bot = dot(x_ref[rows + base + start : rows + base + stop, :], q_bot, (1, 0))
         packed_store(span(refs, start, stop), slice(None), top, bot, half)
+
+
+def rounded_factor(s_ref, s):
+    h, cols = s_ref.shape
+    packed_store(s_ref, slice(None), *pack_window(s[:h], s[h : 2 * h], cols // 2), cols // 2)
+
+
+def factor(s_ref):
+    s = unpack_window(s_ref[...].astype(F32))
+    half, w = s.shape
+    lane = lax.broadcasted_iota(jnp.int32, s.shape, 1)
+    return filled(jnp.where(lane >= w - half, s, 0.0)), half
+
+
+def left_pair(s, half):
+    left = left_columns(s, half)
+    return left, moved(left, s.shape[1] - half)
 
 
 def rotor_kernel(n_parts, *refs):
     parts = refs[:n_parts]
     x_ref, s_ref, *a_refs = refs[n_parts:]
-    half = s_ref.shape[0]
     s = cross_of(parts)
-    left = left_columns(s, half)
-    rotate_into(a_refs, x_ref, left, moved(left, s.shape[1] - half))
-    s_ref[...] = s[:half]
+    rounded_factor(s_ref, s)
+    rotate_into(a_refs, x_ref, *left_pair(low(s).astype(F32), x_ref.shape[1] // 2))
 
 
 def rotor(parts, x, sizes):
-    rows, cols = x.shape
+    _, cols = x.shape
     w = window(cols // 2)
     s, *a = pl.pallas_call(
         functools.partial(rotor_kernel, len(parts)),
         in_specs=whole(len(parts) + 1),
         out_specs=whole(1 + len(sizes)),
-        out_shape=[jax.ShapeDtypeStruct((cols // 2, w), F32)] + blocks_of(cols, sizes),
-        cost_estimate=pl.CostEstimate(flops=2 * rows * cols * w, bytes_accessed=3 * rows * cols, transcendentals=0),
+        out_shape=blocks_of(cols, [cols // 4] + sizes),
+        cost_estimate=pl.CostEstimate(flops=4 * sum(sizes) * cols * w, bytes_accessed=6 * sum(sizes) * cols, transcendentals=0),
         compiler_params=params(),
         name="rotor",
     )(*parts, x)
     return s, a
 
 
+def tail_kernel(s_ref, x_ref, a_ref):
+    rotate_into([a_ref], x_ref, *left_pair(*factor(s_ref)), base=x_ref.shape[0] // 2 - a_ref.shape[0])
+
+
+def tail(s, x, k):
+    cols = x.shape[1]
+    w = window(cols // 2)
+    return pl.pallas_call(
+        tail_kernel,
+        in_specs=whole(2),
+        out_specs=whole(1)[0],
+        out_shape=jax.ShapeDtypeStruct((k, cols), BF16),
+        cost_estimate=pl.CostEstimate(flops=4 * k * cols * w, bytes_accessed=6 * k * cols, transcendentals=0),
+        compiler_params=params(),
+        name="tail",
+    )(s, x)
+
+
 def rotate_kernel(s_ref, x_ref, *b_refs):
-    half = s_ref.shape[0]
-    right = right_columns(filled(s_ref[...]), half)
+    s, half = factor(s_ref)
+    right = right_columns(s, half)
     rotate_into(b_refs, x_ref, moved(right, half), right)
 
 
 def rotate(s, x, sizes):
     rows, cols = x.shape
-    w = s.shape[1]
+    w = window(cols // 2)
     return pl.pallas_call(
         rotate_kernel,
         in_specs=whole(2),
@@ -290,10 +340,9 @@
 def second_kernel(n_parts, *refs):
     parts = refs[:n_parts]
     s_ref, left_ref = refs[n_parts:]
-    h, cols = s_ref.shape
     s = cross_of(parts)
-    packed_store(s_ref, slice(None), *pack_window(s[:h], s[h : 2 * h], cols // 2), cols // 2)
-    left_ref[...] = left_columns(s, cols // 2)
+    rounded_factor(s_ref, s)
+    left_ref[...] = left_columns(low(s).astype(F32), s_ref.shape[1] // 2)
 
 
 def second(parts):
@@ -311,10 +360,7 @@
 
 
 def right_kernel(s_ref, right_ref):
-    s = unpack_window(s_ref[...].astype(F32))
-    half, w = s.shape
-    lane = lax.broadcasted_iota(jnp.int32, s.shape, 1)
-    right_ref[...] = right_columns(filled(jnp.where(lane >= w - half, s, 0.0)), half)
+    right_ref[...] = right_columns(*factor(s_ref))
 
 
 def right_of(s):
@@ -371,17 +417,21 @@
     )(*a, *b, q)
 
 
-def final_kernel(n_a, n_b, *refs):
-    a_refs, b_refs, (l_ref, q_ref, o_hbm, o_ref, sem) = refs[:n_a], refs[n_a : n_a + n_b], refs[n_a + n_b :]
-    rows, cols = o_ref.shape[0] // 2, o_ref.shape[1]
+def final_kernel(base, cuts, n_a, *refs):
+    a_refs, (b_ref, l_ref, q_ref, *_, o_hbm, o_ref, sem) = refs[:n_a], refs[n_a:]
+    rows, cols = l_ref.shape[0] // 2, o_ref.shape[1]
     copies = []
     for first in (True, False):
         weight = pair_weight(q_ref, first)
-        for start, stop in spans(a_refs, b_refs):
+        for start, stop in cuts:
+            a, b = span(a_refs, start, stop), b_ref.at[start - base : stop - base]
+            right = pair_dot([a], [b], 0, stop - start, weight, first)
             to = slice(start, stop) if first else slice(rows + start, rows + stop)
-            right = pair_dot(a_refs, b_refs, start, stop, weight, first)
-            packed_store(o_ref, to, l_ref[to, :].astype(F32), right, cols // 2)
-            copy = pltpu.make_async_copy(o_ref.at[to, :], o_hbm.at[to, :], sem.at[len(copies)])
+            shift = -base if first else b_ref.shape[0] - base
+            here = slice(start + shift, stop + shift)
+            left = l_ref[to, :].astype(F32)
+            packed_store(o_ref, here, left, right, cols // 2)
+            copy = pltpu.make_async_copy(o_ref.at[here, :], o_hbm.at[to, :], sem.at[len(copies)])
             copy.start()
             copies.append(copy)
     for copy in copies:
@@ -391,21 +441,31 @@
 def final(l, a, b, q):
     rows, cols = l.shape[0], a[0].shape[1]
     w = q.shape[1]
-    return pl.pallas_call(
-        functools.partial(final_kernel, len(a), len(b)),
-        in_specs=whole(len(a) + len(b) + 2),
-        out_specs=pl.BlockSpec(memory_space=pl.ANY),
-        out_shape=jax.ShapeDtypeStruct((rows, cols), BF16),
-        scratch_shapes=[pltpu.VMEM((rows, cols), BF16), pltpu.SemaphoreType.DMA((2 * len(spans(a, b)),))],
-        cost_estimate=pl.CostEstimate(flops=4 * rows * w * w, bytes_accessed=4 * rows * cols, transcendentals=0),
-        compiler_params=params(),
-        name="final",
-    )(*a, *b, l, q)
-
-
-def shifted(x, axis, by):
-    n = lax.axis_size(axis)
-    return lax.ppermute(x, axis, [(i, (i + by) % n) for i in range(n)])
+    out, base = [], 0
+    for block in b:
+        n = block.shape[0]
+        cuts = [(i, j) for i, j in spans(a, b) if base <= i < base + n]
+        args = (*a, block, l, q, *out)
+        out = [
+            pl.pallas_call(
+                functools.partial(final_kernel, base, cuts, len(a)),
+                in_specs=whole(len(a) + 3) + [pl.BlockSpec(memory_space=pltpu.HBM)] * len(out),
+                out_specs=pl.BlockSpec(memory_space=pltpu.HBM),
+                out_shape=jax.ShapeDtypeStruct((rows, cols), BF16),
+                input_output_aliases={len(args) - 1: 0} if out else {},
+                scratch_shapes=[pltpu.VMEM((2 * n, cols), BF16), pltpu.SemaphoreType.DMA((2 * len(cuts),))],
+                cost_estimate=pl.CostEstimate(flops=8 * n * w * w, bytes_accessed=8 * n * cols, transcendentals=0),
+                compiler_params=params(),
+                name="final",
+            )(*args)
+        ]
+        base += n
+    return out[0]
+
+
+def passed(x, by):
+    n = lax.axis_size("pairs")
+    return lax.ppermute(x, "pairs", [(i, (i + 2 * by) % n) for i in range(n)])
 
 
 def row_parts(g):
@@ -415,22 +475,28 @@
     return [g] + [lax.ppermute(g, "rows", [(i, i ^ k) for i in range(n)]) for k in range(1, n)]
 
 
-def shares(rows, *eighths):
-    return [rows * e // 8 for e in eighths]
+def shares(rows, *parts):
+    return [rows * e // 64 for e in parts]
 
 
 def local(latent):
     rows = latent.shape[0] // 2
-    stats, latent = gram(latent, 4)
-    s, a = rotor(row_parts(stats), latent, shares(rows, 7, 1))
-    a_in = [shifted(v, "pairs", 2) for v in a]
-    b = rotate(s, latent, shares(rows, 5, 3))
+    head, middle, last = shares(rows, 36, 8, 20)
+    raw_in = passed(taken(latent, last), 1)
+    parts = row_parts(gram(latent, 4))
+    s, a = rotor(parts, latent, [head, middle])
+    s_in = passed(s, 1)
+    a_in = [passed(a[0], 1)]
+    a_in.append(passed(a[1], 1))
+    b = rotate(s, latent, shares(rows, 44, 20))
+    a.append(tail(s, latent, last))
+    a_in.append(tail(s_in, raw_in, last))
     a_in[0], b_out = lax.optimization_barrier((a_in[0], b[0]))
-    b_in = [shifted(b_out, "pairs", -2)]
+    b_in = [passed(b_out, -1)]
     s, left = second(row_parts(gram_pair(a_in, b)))
-    s_in = shifted(s, "pairs", -2)
+    s_in = passed(s, -1)
     left, b_out = lax.optimization_barrier((left, b[1]))
-    b_in.append(shifted(b_out, "pairs", -2))
+    b_in.append(passed(b_out, -1))
     return final(left_half(a_in, b, left), a, b_in, right_of(s_in))
 
 

time: 54.8 us -> 73.1 us (1.33)
  waiting for transfers between devices: 29.2 us -> 42.2 us
  Pallas kernels: 10.8 us -> 13.6 us
  local copies, waits for them, and re-layouts: 0 us -> 1.41 us
  starting transfers between devices: 14.6 us -> 15.6 us
    ppermute x5 -> x7, waiting for transfers between devices: 21.5 us -> 34 us  [passed(): return lax.ppermute(x, 'pairs', [(i, (i + 2 * by) % n) for i in range(n)])]
    pallas_call x2 -> x6, Pallas kernels: 3.93 us -> 6.69 us  [the longest x2 2.61 us: final(): pl.pallas_call(functools.partial(final_kernel, base, cuts, len(a)), in_sp...]
    unnamed x0 -> x4, local copies, waits for them, and re-layouts: none -> 1.41 us
    ppermute x5 -> x7, starting transfers between devices: 6.38 us -> 7.46 us  [passed(): return lax.ppermute(x, 'pairs', [(i, (i + 2 * by) % n) for i in range(n)])]
  transfers between devices with their start and end apart: 11 -> 13, of which waited for: 9 -> 9; matrix products, arithmetic and copies ran while one was open for 0% -> 0% of each run, Pallas kernels for 9% -> 14%
where the time goes in v2:
time: 73.1 us; the launch traced here: 72.9 us
  waiting for transfers between devices  42.2 us (58%)
  starting transfers between devices  15.6 us (21%)
  Pallas kernels  13.6 us (19%)
  local copies, waits for them, and re-layouts  1.41 us (2%)
    ppermute x7, waiting for transfers between devices, passed(): return lax.ppermute(x, 'pairs', [(i, (i + 2 * by) % n) for i in range(n)])  34 us
    ppermute x6, waiting for transfers between devices, row_parts(): lax.ppermute(g, 'rows', [(i, i ^ k) for i in range(n)])  8.19 us
    ppermute x6, starting transfers between devices, row_parts(): lax.ppermute(g, 'rows', [(i, i ^ k) for i in range(n)])  8.18 us
    ppermute x7, starting transfers between devices, passed(): return lax.ppermute(x, 'pairs', [(i, (i + 2 * by) % n) for i in range(n)])  7.46 us
    pallas_call x2, Pallas kernels, final(): pl.pallas_call(functools.partial(final_kernel, base, cuts, len(a)), in_sp...  2.61 us
    pallas_call x2, Pallas kernels, tail(): pl.pallas_call(tail_kernel, in_specs=whole(2), out_specs=whole(1)[0], out...  2.48 us
    pallas_call x1, Pallas kernels, rotor(): pl.pallas_call(functools.partial(rotor_kernel, len(parts)), in_specs=whol...  1.75 us
    pallas_call x1, Pallas kernels, rotate(): pl.pallas_call(rotate_kernel, in_specs=whole(2), out_specs=whole(len(size...  1.6 us
  transfers between devices with their start and end apart: 13, of which 9 were waited for; matrix products, arithmetic and copies ran while one was open for 0% of the time, Pallas kernels for 14%

profile of v2, /device:TPU:0, one launch (start us, length us, event | category | flops | bytes accessed | tf_op | source)
XLA Modules:
  0.0 72.9 jit_solution(16576281501276235034)
XLA Ops:
  0.0 0.0 copy-start
  0.0 1.4 %copy-done = bf16[2048,384]{1,0:T(8,128)(2,1)S(1)} copy-done((bf16[2048,384]{1,0:T(8,128)(2,1)S(1)}, bf16[2048,384]{1,0:T(8,128)(2,1)}, u32[]{:S(2)}) %copy-start) | copy-done | bytes 1572888
  1.4 0.5 gram.1.refs_0_
  1.9 0.0 copy-start.1
  2.0 4.0 %collective-permute-start.2 = (bf16[104,384]{1,0:T(8,128)(2,1)S(1)}, bf16[104,384]{1,0:T(8,128)(2,1)S(1)}, u32[]{:S(2)}, u32[]{:S(2)}) collective-permute-start(bf16[104,384]{1,0:T(8,128)(2,1)S(1)} %gram.1.refs_0_), channel_id=1, source_target_pairs={{0,24},{8,16},{16,8},{24,0},{1,25},{9,17},{17,9},{25,1},{2,26},{10... | collective-permute-start | bytes 239624 | tf_op jit(solution)/shard_map/ppermute | solution.py:475
  5.9 0.5 collective-permute-start.1
  6.5 0.1 collective-permute-start
  6.6 1.9 %collective-permute-done.2.refs_3_ = bf16[104,384]{1,0:T(8,128)(2,1)S(1)} collective-permute-done((bf16[104,384]{1,0:T(8,128)(2,1)S(1)}, bf16[104,384]{1,0:T(8,128)(2,1)S(1)}, u32[]{:S(2)}, u32[]{:S(2)}) %collective-permute-start.2) | collective-permute-done | bytes 79904 | tf_op jit(solution)/shard_map/ppermute | solution.py:475
  8.5 1.9 %collective-permute-done.1.refs_2_ = bf16[104,384]{1,0:T(8,128)(2,1)S(1)} collective-permute-done((bf16[104,384]{1,0:T(8,128)(2,1)S(1)}, bf16[104,384]{1,0:T(8,128)(2,1)S(1)}, u32[]{:S(2)}, u32[]{:S(2)}) %collective-permute-start.1) | collective-permute-done | bytes 79904 | tf_op jit(solution)/shard_map/ppermute | solution.py:475
  10.4 0.5 collective-permute-done.refs_1_
  10.9 1.8 %rotor.1 = (bf16[96,384]{1,0:T(8,128)(2,1)S(1)}, bf16[576,384]{1,0:T(8,128)(2,1)S(1)}, bf16[128,384]{1,0:T(8,128)(2,1)S(1)}) custom-call(bf16[104,384]{1,0:T(8,128)(2,1)S(1)} %gram.1.refs_0_, bf16[104,384]{1,0:T(8,128)(2,1)S(1)} %collective-permute-done.refs_1_, bf16[104,384]{1,0:T(8,128)(2,1)S(1)} %collective-permute-done.1.refs_2_, ...), custom_call_target="tpu_custom_call" | custom-call | flops 276824064 | bytes 1622016 | tf_op jit(solution)/shard_map/rotor/pallas_call | solution.py:290
  12.6 1.6 %collective-permute-start.3 = (bf16[576,384]{1,0:T(8,128)(2,1)S(1)}, bf16[576,384]{1,0:T(8,128)(2,1)S(1)}, u32[]{:S(2)}, u32[]{:S(2)}) collective-permute-start(bf16[576,384]{1,0:T(8,128)(2,1)S(1)} %get-tuple-element.16.refs_0_), channel_id=1, source_target_pairs={{0,2},{1,3},{2,4},{3,5},{4,6},{5,7},{6,0},{7,1},{8,10},{9,11},{10,... | collective-permute-start | bytes 1327112 | tf_op jit(solution)/shard_map/ppermute | solution.py:468
  14.3 1.1 %taken.1 = bf16[640,384]{1,0:T(8,128)(2,1)S(1)} custom-call(bf16[2048,384]{1,0:T(8,128)(2,1)} %x_hbm.1), custom_call_target="tpu_custom_call" | custom-call | bytes 983040 | tf_op jit(solution)/shard_map/taken/pallas_call | solution.py:113
  15.3 1.6 %collective-permute-start.6 = (bf16[640,384]{1,0:T(8,128)(2,1)S(1)}, bf16[640,384]{1,0:T(8,128)(2,1)S(1)}, u32[]{:S(2)}, u32[]{:S(2)}) collective-permute-start(bf16[640,384]{1,0:T(8,128)(2,1)S(1)} %taken.1), channel_id=1, source_target_pairs={{0,2},{1,3},{2,4},{3,5},{4,6},{5,7},{6,0},{7,1},{8,10},{9,11},{10,... | collective-permute-start | bytes 1474568 | tf_op jit(solution)/shard_map/ppermute | solution.py:468
  17.0 0.0 copy-done.1
  17.0 1.6 %rotate.1 = (bf16[704,384]{1,0:T(8,128)(2,1)S(1)}, bf16[320,384]{1,0:T(8,128)(2,1)S(1)}) custom-call(bf16[96,384]{1,0:T(8,128)(2,1)S(1)} %get-tuple-element.18.s_ref, bf16[2048,384]{1,0:T(8,128)(2,1)S(1)} %copy-done.1), custom_call_target="tpu_custom_call" | custom-call | flops 402653184 | bytes 2359296 | tf_op jit(solution)/shard_map/rotate/pallas_call | solution.py:329
  18.6 9.1 %collective-permute-done.3.refs_0_ = bf16[576,384]{1,0:T(8,128)(2,1)S(1)} collective-permute-done((bf16[576,384]{1,0:T(8,128)(2,1)S(1)}, bf16[576,384]{1,0:T(8,128)(2,1)S(1)}, u32[]{:S(2)}, u32[]{:S(2)}) %collective-permute-start.3) | collective-permute-done | bytes 442400 | tf_op jit(solution)/shard_map/ppermute | solution.py:468
  27.7 1.6 %collective-permute-start.12 = (bf16[704,384]{1,0:T(8,128)(2,1)S(1)}, bf16[704,384]{1,0:T(8,128)(2,1)S(1)}, u32[]{:S(2)}, u32[]{:S(2)}) collective-permute-start(bf16[704,384]{1,0:T(8,128)(2,1)S(1)} %get-tuple-element.26.refs_3_), channel_id=1, source_target_pairs={{0,6},{1,7},{2,0},{3,1},{4,2},{5,3},{6,4},{7,5},{8,14},{9,15},{10,... | collective-permute-start | bytes 1622024 | tf_op jit(solution)/shard_map/ppermute | solution.py:468
  29.3 0.4 collective-permute-start.4
  29.7 0.0 collective-permute-start.5
  29.8 21.8 %collective-permute-done.5.s_ref = bf16[96,384]{1,0:T(8,128)(2,1)S(1)} collective-permute-done((bf16[96,384]{1,0:T(8,128)(2,1)S(1)}, bf16[96,384]{1,0:T(8,128)(2,1)S(1)}, u32[]{:S(2)}, u32[]{:S(2)}) %collective-permute-start.5) | collective-permute-done | bytes 73760 | tf_op jit(solution)/shard_map/ppermute | solution.py:468
  51.6 0.0 collective-permute-done.6.x_ref
  51.6 1.2 %tail.3.refs_2_ = bf16[320,384]{1,0:T(8,128)(2,1)S(1)} custom-call(bf16[96,384]{1,0:T(8,128)(2,1)S(1)} %collective-permute-done.5.s_ref, bf16[640,384]{1,0:T(8,128)(2,1)S(1)} %collective-permute-done.6.x_ref), custom_call_target="tpu_custom_call" | custom-call | flops 125829120 | bytes 737280 | tf_op jit(solution)/shard_map/tail/pallas_call | solution.py:309
  52.8 0.0 collective-permute-done.4.refs_1_
  52.9 0.7 %gram_pair.1.refs_0_ = bf16[104,384]{1,0:T(8,128)(2,1)S(1)} custom-call(bf16[576,384]{1,0:T(8,128)(2,1)S(1)} %collective-permute-done.3.refs_0_, bf16[128,384]{1,0:T(8,128)(2,1)S(1)} %collective-permute-done.4.refs_1_, bf16[320,384]{1,0:T(8,128)(2,1)S(1)} %tail.3.refs_2_, bf16[704,384]{1,0:T(8,128)(2,1)S(1)} %get-tuple-element.26.refs_3_, ...), custom_call_target="tpu_custom_call" | custom-call | flops 268435456 | bytes 1572864 | tf_op jit(solution)/shard_map/gram_pair/pallas_call | solution.py:179
  53.6 1.4 %collective-permute-start.9 = (bf16[104,384]{1,0:T(8,128)(2,1)S(1)}, bf16[104,384]{1,0:T(8,128)(2,1)S(1)}, u32[]{:S(2)}, u32[]{:S(2)}) collective-permute-start(bf16[104,384]{1,0:T(8,128)(2,1)S(1)} %gram_pair.1.refs_0_), channel_id=1, source_target_pairs={{0,24},{8,16},{16,8},{24,0},{1,25},{9,17},{17,9},{25,1},{2,26},{10... | collective-permute-start | bytes 239624 | tf_op jit(solution)/shard_map/ppermute | solution.py:475
  55.0 1.6 %collective-permute-start.8 = (bf16[104,384]{1,0:T(8,128)(2,1)S(1)}, bf16[104,384]{1,0:T(8,128)(2,1)S(1)}, u32[]{:S(2)}, u32[]{:S(2)}) collective-permute-start(bf16[104,384]{1,0:T(8,128)(2,1)S(1)} %gram_pair.1.refs_0_), channel_id=1, source_target_pairs={{0,16},{8,24},{16,0},{24,8},{1,17},{9,25},{17,1},{25,9},{2,18},{10... | collective-permute-start | bytes 239624 | tf_op jit(solution)/shard_map/ppermute | solution.py:475
  56.6 0.5 collective-permute-start.7
  57.2 1.9 %collective-permute-done.9.refs_3_ = bf16[104,384]{1,0:T(8,128)(2,1)S(1)} collective-permute-done((bf16[104,384]{1,0:T(8,128)(2,1)S(1)}, bf16[104,384]{1,0:T(8,128)(2,1)S(1)}, u32[]{:S(2)}, u32[]{:S(2)}) %collective-permute-start.9) | collective-permute-done | bytes 79904 | tf_op jit(solution)/shard_map/ppermute | solution.py:475
  59.0 0.8 %collective-permute-done.8.refs_2_ = bf16[104,384]{1,0:T(8,128)(2,1)S(1)} collective-permute-done((bf16[104,384]{1,0:T(8,128)(2,1)S(1)}, bf16[104,384]{1,0:T(8,128)(2,1)S(1)}, u32[]{:S(2)}, u32[]{:S(2)}) %collective-permute-start.8) | collective-permute-done | bytes 79904 | tf_op jit(solution)/shard_map/ppermute | solution.py:475
  59.8 1.2 %collective-permute-done.7.refs_1_ = bf16[104,384]{1,0:T(8,128)(2,1)S(1)} collective-permute-done((bf16[104,384]{1,0:T(8,128)(2,1)S(1)}, bf16[104,384]{1,0:T(8,128)(2,1)S(1)}, u32[]{:S(2)}, u32[]{:S(2)}) %collective-permute-start.7) | collective-permute-done | bytes 79904 | tf_op jit(solution)/shard_map/ppermute | solution.py:475
  61.1 1.2 %second.1 = (bf16[96,384]{1,0:T(8,128)(2,1)S(1)}, bf16[384,256]{1,0:T(8,128)(2,1)S(1)}) custom-call(bf16[104,384]{1,0:T(8,128)(2,1)S(1)} %gram_pair.1.refs_0_, bf16[104,384]{1,0:T(8,128)(2,1)S(1)} %collective-permute-done.7.refs_1_, bf16[104,384]{1,0:T(8,128)(2,1)S(1)} %collective-permute-done.8.refs_2_, bf16[104,384]{1,0:T(8,128)(2,1)S(1)} %collective-permute-done.9.refs_3_), custom_call_target="tpu_custom_call" | custom-call | flops 134217728 | bytes 262144 | tf_op jit(solution)/shard_map/second/pallas_call | solution.py:351
  62.3 1.7 %collective-permute-start.10 = (bf16[320,384]{1,0:T(8,128)(2,1)S(1)}, bf16[320,384]{1,0:T(8,128)(2,1)S(1)}, u32[]{:S(2)}, u32[]{:S(2)}) collective-permute-start(bf16[320,384]{1,0:T(8,128)(2,1)S(1)} %get-tuple-element.23.refs_4_), channel_id=1, source_target_pairs={{0,6},{1,7},{2,0},{3,1},{4,2},{5,3},{6,4},{7,5},{8,14},{9,15},{10,... | collective-permute-start | bytes 737288 | tf_op jit(solution)/shard_map/ppermute | solution.py:468
  64.0 0.4 collective-permute-start.11
  64.5 1.2 %tail.2.refs_2_ = bf16[320,384]{1,0:T(8,128)(2,1)S(1)} custom-call(bf16[96,384]{1,0:T(8,128)(2,1)S(1)} %get-tuple-element.18.s_ref, bf16[2048,384]{1,0:T(8,128)(2,1)S(1)} %copy-done.1), custom_call_target="tpu_custom_call" | custom-call | flops 125829120 | bytes 737280 | tf_op jit(solution)/shard_map/tail/pallas_call | solution.py:309
  65.7 0.7 left_half.1.refs_4_
  66.4 3.0 %collective-permute-done.11.s_ref = bf16[96,384]{1,0:T(8,128)(2,1)S(1)} collective-permute-done((bf16[96,384]{1,0:T(8,128)(2,1)S(1)}, bf16[96,384]{1,0:T(8,128)(2,1)S(1)}, u32[]{:S(2)}, u32[]{:S(2)}) %collective-permute-start.11) | collective-permute-done | bytes 73760 | tf_op jit(solution)/shard_map/ppermute | solution.py:468
  69.4 0.9 %right.1.refs_5_ = bf16[384,256]{1,0:T(8,128)(2,1)S(1)} custom-call(bf16[96,384]{1,0:T(8,128)(2,1)S(1)} %collective-permute-done.11.s_ref), custom_call_target="tpu_custom_call" | custom-call | flops 134217728 | bytes 262144 | tf_op jit(solution)/shard_map/right/pallas_call | solution.py:369
  70.3 0.0 collective-permute-done.12.refs_3_
  70.3 1.5 %final.2.refs_6_ = bf16[2048,384]{1,0:T(8,128)(2,1)} custom-call(bf16[576,384]{1,0:T(8,128)(2,1)S(1)} %get-tuple-element.16.refs_0_, bf16[128,384]{1,0:T(8,128)(2,1)S(1)} %get-tuple-element.17.refs_1_, bf16[320,384]{1,0:T(8,128)(2,1)S(1)} %tail.2.refs_2_, bf16[704,384]{1,0:T(8,128)(2,1)S(1)} %collective-permute-done.12.refs_3_, ...), custom_call_target="tpu_custom_call" | custom-call | flops 369098752 | bytes 2162688 | tf_op jit(solution)/shard_map/final/pallas_call | solution.py:450
  71.8 0.0 collective-permute-done.10.refs_3_
  71.8 1.1 %final.3 = bf16[2048,384]{1,0:T(8,128)(2,1)} custom-call(bf16[576,384]{1,0:T(8,128)(2,1)S(1)} %get-tuple-element.16.refs_0_, bf16[128,384]{1,0:T(8,128)(2,1)S(1)} %get-tuple-element.17.refs_1_, bf16[320,384]{1,0:T(8,128)(2,1)S(1)} %tail.2.refs_2_, bf16[320,384]{1,0:T(8,128)(2,1)S(1)} %collective-permute-done.10.refs_3_, ...), custom_call_target="tpu_custom_call", output_to_operand_aliasing={{}: (6, {})} | custom-call | flops 167772160 | bytes 983040 | tf_op jit(solution)/shard_map/final/pallas_call | solution.py:450
Async XLA Ops:
  0.0 1.4 %copy-start = (bf16[2048,384]{1,0:T(8,128)(2,1)S(1)}, bf16[2048,384]{1,0:T(8,128)(2,1)}, u32[]{:S(2)}) copy-start(bf16[2048,384]{1,0:T(8,128)(2,1)} %x_hbm.1) | copy-start | bytes 4718596
  1.9 15.0 %copy-start.1 = (bf16[2048,384]{1,0:T(8,128)(2,1)S(1)}, bf16[2048,384]{1,0:T(8,128)(2,1)}, u32[]{:S(2)}) copy-start(bf16[2048,384]{1,0:T(8,128)(2,1)} %x_hbm.1) | copy-start | bytes 4718596
  2.0 6.5 %collective-permute-start.2 = (bf16[104,384]{1,0:T(8,128)(2,1)S(1)}, bf16[104,384]{1,0:T(8,128)(2,1)S(1)}, u32[]{:S(2)}, u32[]{:S(2)}) collective-permute-start(bf16[104,384]{1,0:T(8,128)(2,1)S(1)} %gram.1.refs_0_), channel_id=1, source_target_pairs={{0,24},{8,16},{16,8},{24,0},{1,25},{9,17},{17,9},{25,1},{2,26},{10... | collective-permute-start | bytes 239624 | tf_op jit(solution)/shard_map/ppermute | solution.py:475
  5.9 4.4 %collective-permute-start.1 = (bf16[104,384]{1,0:T(8,128)(2,1)S(1)}, bf16[104,384]{1,0:T(8,128)(2,1)S(1)}, u32[]{:S(2)}, u32[]{:S(2)}) collective-permute-start(bf16[104,384]{1,0:T(8,128)(2,1)S(1)} %gram.1.refs_0_), channel_id=1, source_target_pairs={{0,16},{8,24},{16,0},{24,8},{1,17},{9,25},{17,1},{25,9},{2,18},{10... | collective-permute-start | bytes 239624 | tf_op jit(solution)/shard_map/ppermute | solution.py:475
  6.5 4.4 %collective-permute-start = (bf16[104,384]{1,0:T(8,128)(2,1)S(1)}, bf16[104,384]{1,0:T(8,128)(2,1)S(1)}, u32[]{:S(2)}, u32[]{:S(2)}) collective-permute-start(bf16[104,384]{1,0:T(8,128)(2,1)S(1)} %gram.1.refs_0_), channel_id=1, source_target_pairs={{0,8},{8,0},{16,24},{24,16},{1,9},{9,1},{17,25},{25,17},{2,10},{10... | collective-permute-start | bytes 239624 | tf_op jit(solution)/shard_map/ppermute | solution.py:475
  12.6 15.1 %collective-permute-start.3 = (bf16[576,384]{1,0:T(8,128)(2,1)S(1)}, bf16[576,384]{1,0:T(8,128)(2,1)S(1)}, u32[]{:S(2)}, u32[]{:S(2)}) collective-permute-start(bf16[576,384]{1,0:T(8,128)(2,1)S(1)} %get-tuple-element.16.refs_0_), channel_id=1, source_target_pairs={{0,2},{1,3},{2,4},{3,5},{4,6},{5,7},{6,0},{7,1},{8,10},{9,11},{10,... | collective-permute-start | bytes 1327112 | tf_op jit(solution)/shard_map/ppermute | solution.py:468
  15.3 36.2 %collective-permute-start.6 = (bf16[640,384]{1,0:T(8,128)(2,1)S(1)}, bf16[640,384]{1,0:T(8,128)(2,1)S(1)}, u32[]{:S(2)}, u32[]{:S(2)}) collective-permute-start(bf16[640,384]{1,0:T(8,128)(2,1)S(1)} %taken.1), channel_id=1, source_target_pairs={{0,2},{1,3},{2,4},{3,5},{4,6},{5,7},{6,0},{7,1},{8,10},{9,11},{10,... | collective-permute-start | bytes 1474568 | tf_op jit(solution)/shard_map/ppermute | solution.py:468
  27.7 42.6 %collective-permute-start.12 = (bf16[704,384]{1,0:T(8,128)(2,1)S(1)}, bf16[704,384]{1,0:T(8,128)(2,1)S(1)}, u32[]{:S(2)}, u32[]{:S(2)}) collective-permute-start(bf16[704,384]{1,0:T(8,128)(2,1)S(1)} %get-tuple-element.26.refs_3_), channel_id=1, source_target_pairs={{0,6},{1,7},{2,0},{3,1},{4,2},{5,3},{6,4},{7,5},{8,14},{9,15},{10,... | collective-permute-start | bytes 1622024 | tf_op jit(solution)/shard_map/ppermute | solution.py:468
  29.3 23.5 %collective-permute-start.4 = (bf16[128,384]{1,0:T(8,128)(2,1)S(1)}, bf16[128,384]{1,0:T(8,128)(2,1)S(1)}, u32[]{:S(2)}, u32[]{:S(2)}) collective-permute-start(bf16[128,384]{1,0:T(8,128)(2,1)S(1)} %get-tuple-element.17.refs_1_), channel_id=1, source_target_pairs={{0,2},{1,3},{2,4},{3,5},{4,6},{5,7},{6,0},{7,1},{8,10},{9,11},{10,... | collective-permute-start | bytes 294920 | tf_op jit(solution)/shard_map/ppermute | solution.py:468
  29.7 21.9 %collective-permute-start.5 = (bf16[96,384]{1,0:T(8,128)(2,1)S(1)}, bf16[96,384]{1,0:T(8,128)(2,1)S(1)}, u32[]{:S(2)}, u32[]{:S(2)}) collective-permute-start(bf16[96,384]{1,0:T(8,128)(2,1)S(1)} %get-tuple-element.18.s_ref), channel_id=1, source_target_pairs={{0,2},{1,3},{2,4},{3,5},{4,6},{5,7},{6,0},{7,1},{8,10},{9,11},{10,... | collective-permute-start | bytes 221192 | tf_op jit(solution)/shard_map/ppermute | solution.py:468
  53.6 5.4 %collective-permute-start.9 = (bf16[104,384]{1,0:T(8,128)(2,1)S(1)}, bf16[104,384]{1,0:T(8,128)(2,1)S(1)}, u32[]{:S(2)}, u32[]{:S(2)}) collective-permute-start(bf16[104,384]{1,0:T(8,128)(2,1)S(1)} %gram_pair.1.refs_0_), channel_id=1, source_target_pairs={{0,24},{8,16},{16,8},{24,0},{1,25},{9,17},{17,9},{25,1},{2,26},{10... | collective-permute-start | bytes 239624 | tf_op jit(solution)/shard_map/ppermute | solution.py:475
  55.0 4.8 %collective-permute-start.8 = (bf16[104,384]{1,0:T(8,128)(2,1)S(1)}, bf16[104,384]{1,0:T(8,128)(2,1)S(1)}, u32[]{:S(2)}, u32[]{:S(2)}) collective-permute-start(bf16[104,384]{1,0:T(8,128)(2,1)S(1)} %gram_pair.1.refs_0_), channel_id=1, source_target_pairs={{0,16},{8,24},{16,0},{24,8},{1,17},{9,25},{17,1},{25,9},{2,18},{10... | collective-permute-start | bytes 239624 | tf_op jit(solution)/shard_map/ppermute | solution.py:475
  56.6 4.4 %collective-permute-start.7 = (bf16[104,384]{1,0:T(8,128)(2,1)S(1)}, bf16[104,384]{1,0:T(8,128)(2,1)S(1)}, u32[]{:S(2)}, u32[]{:S(2)}) collective-permute-start(bf16[104,384]{1,0:T(8,128)(2,1)S(1)} %gram_pair.1.refs_0_), channel_id=1, source_target_pairs={{0,8},{8,0},{16,24},{24,16},{1,9},{9,1},{17,25},{25,17},{2,10},{10... | collective-permute-start | bytes 239624 | tf_op jit(solution)/shard_map/ppermute | solution.py:475
  62.3 9.5 %collective-permute-start.10 = (bf16[320,384]{1,0:T(8,128)(2,1)S(1)}, bf16[320,384]{1,0:T(8,128)(2,1)S(1)}, u32[]{:S(2)}, u32[]{:S(2)}) collective-permute-start(bf16[320,384]{1,0:T(8,128)(2,1)S(1)} %get-tuple-element.23.refs_4_), channel_id=1, source_target_pairs={{0,6},{1,7},{2,0},{3,1},{4,2},{5,3},{6,4},{7,5},{8,14},{9,15},{10,... | collective-permute-start | bytes 737288 | tf_op jit(solution)/shard_map/ppermute | solution.py:468
  64.0 5.4 %collective-permute-start.11 = (bf16[96,384]{1,0:T(8,128)(2,1)S(1)}, bf16[96,384]{1,0:T(8,128)(2,1)S(1)}, u32[]{:S(2)}, u32[]{:S(2)}) collective-permute-start(bf16[96,384]{1,0:T(8,128)(2,1)S(1)} %get-tuple-element.25), channel_id=1, source_target_pairs={{0,6},{1,7},{2,0},{3,1},{4,2},{5,3},{6,4},{7,5},{8,14},{9,15},{10,... | collective-permute-start | bytes 221192 | tf_op jit(solution)/shard_map/ppermute | solution.py:468

commit v3 on v2

--- a/solution.py
+++ b/solution.py
@@ -264,8 +264,35 @@
     packed_store(s_ref, slice(None), *pack_window(s[:h], s[h : 2 * h], cols // 2), cols // 2)
 
 
-def factor(s_ref):
-    s = unpack_window(s_ref[...].astype(F32))
+def own_share(s_ref, n):
+    s = s_ref[...].astype(F32)
+    h = s.shape[0] // n
+    me, share = lax.axis_index("rows"), s[:h]
+    for k in range(1, n):
+        share = jnp.where(me == k, s[k * h : (k + 1) * h], share)
+    return low(share)
+
+
+def joined(share_refs):
+    shares = [ref[...].astype(F32) for ref in share_refs]
+    if len(shares) == 1:
+        return shares[0]
+    me, rows = lax.axis_index("rows"), []
+    for at in range(len(shares)):
+        row = shares[0]
+        for k in range(1, len(shares)):
+            row = jnp.where(me == at ^ k, shares[k], row)
+        rows.append(row)
+    return jnp.concatenate(rows, axis=0)
+
+
+def shared(cols):
+    n = lax.axis_size("rows")
+    return n if n <= 4 and not n & (n - 1) and (cols // 4) % (8 * n) == 0 else 1
+
+
+def factor(*share_refs):
+    s = unpack_window(joined(share_refs))
     half, w = s.shape
     lane = lax.broadcasted_iota(jnp.int32, s.shape, 1)
     return filled(jnp.where(lane >= w - half, s, 0.0)), half
@@ -278,29 +305,31 @@
 
 def rotor_kernel(n_parts, *refs):
     parts = refs[:n_parts]
-    x_ref, s_ref, *a_refs = refs[n_parts:]
+    x_ref, s_ref, share_ref, *a_refs = refs[n_parts:]
     s = cross_of(parts)
     rounded_factor(s_ref, s)
+    share_ref[...] = own_share(s_ref, s_ref.shape[0] // share_ref.shape[0])
     rotate_into(a_refs, x_ref, *left_pair(low(s).astype(F32), x_ref.shape[1] // 2))
 
 
 def rotor(parts, x, sizes):
     _, cols = x.shape
     w = window(cols // 2)
-    s, *a = pl.pallas_call(
+    s, share, *a = pl.pallas_call(
         functools.partial(rotor_kernel, len(parts)),
         in_specs=whole(len(parts) + 1),
-        out_specs=whole(1 + len(sizes)),
-        out_shape=blocks_of(cols, [cols // 4] + sizes),
+        out_specs=whole(2 + len(sizes)),
+        out_shape=blocks_of(cols, [cols // 4, cols // 4 // shared(cols)] + sizes),
         cost_estimate=pl.CostEstimate(flops=4 * sum(sizes) * cols * w, bytes_accessed=6 * sum(sizes) * cols, transcendentals=0),
         compiler_params=params(),
         name="rotor",
     )(*parts, x)
-    return s, a
-
-
-def tail_kernel(s_ref, x_ref, a_ref):
-    rotate_into([a_ref], x_ref, *left_pair(*factor(s_ref)), base=x_ref.shape[0] // 2 - a_ref.shape[0])
+    return s, share, a
+
+
+def tail_kernel(*refs):
+    *s_refs, x_ref, a_ref = refs
+    rotate_into([a_ref], x_ref, *left_pair(*factor(*s_refs)), base=x_ref.shape[0] // 2 - a_ref.shape[0])
 
 
 def tail(s, x, k):
@@ -308,13 +337,13 @@
     w = window(cols // 2)
     return pl.pallas_call(
         tail_kernel,
-        in_specs=whole(2),
+        in_specs=whole(len(s) + 1),
         out_specs=whole(1)[0],
         out_shape=jax.ShapeDtypeStruct((k, cols), BF16),
         cost_estimate=pl.CostEstimate(flops=4 * k * cols * w, bytes_accessed=6 * k * cols, transcendentals=0),
         compiler_params=params(),
         name="tail",
-    )(s, x)
+    )(*s, x)
 
 
 def rotate_kernel(s_ref, x_ref, *b_refs):
@@ -481,15 +510,16 @@
 
 def local(latent):
     rows = latent.shape[0] // 2
-    head, middle, last = shares(rows, 36, 8, 20)
+    head, middle, last = shares(rows, 34, 8, 22)
     raw_in = passed(taken(latent, last), 1)
     parts = row_parts(gram(latent, 4))
-    s, a = rotor(parts, latent, [head, middle])
-    s_in = passed(s, 1)
+    s, share, a = rotor(parts, latent, [head, middle])
+    share_in = passed(share, 1)
     a_in = [passed(a[0], 1)]
     a_in.append(passed(a[1], 1))
     b = rotate(s, latent, shares(rows, 44, 20))
-    a.append(tail(s, latent, last))
+    a.append(tail([s], latent, last))
+    s_in = row_parts(share_in) if shared(latent.shape[1]) > 1 else [share_in]
     a_in.append(tail(s_in, raw_in, last))
     a_in[0], b_out = lax.optimization_barrier((a_in[0], b[0]))
     b_in = [passed(b_out, -1)]

time: 73.1 us -> 80.8 us (1.11)
  starting transfers between devices: 15.6 us -> 20.1 us
  waiting for transfers between devices: 42.2 us -> 45.3 us
    ppermute x6 -> x9, starting transfers between devices: 8.18 us -> 12.7 us  [row_parts(): lax.ppermute(g, 'rows', [(i, i ^ k) for i in range(n)])]
    ppermute x6 -> x9, waiting for transfers between devices: 8.19 us -> 12.1 us  [row_parts(): lax.ppermute(g, 'rows', [(i, i ^ k) for i in range(n)])]
  transfers between devices with their start and end apart: 13 -> 16, of which waited for: 9 -> 11; matrix products, arithmetic and copies ran while one was open for 0% -> 0% of each run, Pallas kernels for 14% -> 13%
where the time goes in v3:
time: 80.8 us; the launch traced here: 80.7 us
  waiting for transfers between devices  45.3 us (56%)
  starting transfers between devices  20.1 us (25%)
  Pallas kernels  13.7 us (17%)
  local copies, waits for them, and re-layouts  1.41 us (2%)
    ppermute x7, waiting for transfers between devices, passed(): return lax.ppermute(x, 'pairs', [(i, (i + 2 * by) % n) for i in range(n)])  33.2 us
    ppermute x9, starting transfers between devices, row_parts(): lax.ppermute(g, 'rows', [(i, i ^ k) for i in range(n)])  12.7 us
    ppermute x9, waiting for transfers between devices, row_parts(): lax.ppermute(g, 'rows', [(i, i ^ k) for i in range(n)])  12.1 us
    ppermute x7, starting transfers between devices, passed(): return lax.ppermute(x, 'pairs', [(i, (i + 2 * by) % n) for i in range(n)])  7.46 us
    pallas_call x2, Pallas kernels, final(): pl.pallas_call(functools.partial(final_kernel, base, cuts, len(a)), in_sp...  2.62 us
    pallas_call x2, Pallas kernels, tail(): pl.pallas_call(tail_kernel, in_specs=whole(len(s) + 1), out_specs=whole(1...  2.51 us
    pallas_call x1, Pallas kernels, rotor(): pl.pallas_call(functools.partial(rotor_kernel, len(parts)), in_specs=whol...  1.74 us
  transfers between devices with their start and end apart: 16, of which 11 were waited for; matrix products, arithmetic and copies ran while one was open for 0% of the time, Pallas kernels for 13%

profile of v3, /device:TPU:0, one launch (start us, length us, event | category | flops | bytes accessed | tf_op | source)
XLA Modules:
  0.0 80.7 jit_solution(1613881090434617075)
XLA Ops:
  0.0 0.0 copy-start
  0.0 1.4 %copy-done = bf16[2048,384]{1,0:T(8,128)(2,1)S(1)} copy-done((bf16[2048,384]{1,0:T(8,128)(2,1)S(1)}, bf16[2048,384]{1,0:T(8,128)(2,1)}, u32[]{:S(2)}) %copy-start) | copy-done | bytes 1572888
  1.4 0.5 gram.1.refs_0_
  1.9 0.0 copy-start.1
  2.0 4.0 %collective-permute-start.2 = (bf16[104,384]{1,0:T(8,128)(2,1)S(1)}, bf16[104,384]{1,0:T(8,128)(2,1)S(1)}, u32[]{:S(2)}, u32[]{:S(2)}) collective-permute-start(bf16[104,384]{1,0:T(8,128)(2,1)S(1)} %gram.1.refs_0_), channel_id=1, source_target_pairs={{0,24},{8,16},{16,8},{24,0},{1,25},{9,17},{17,9},{25,1},{2,26},{10... | collective-permute-start | bytes 239624 | tf_op jit(solution)/shard_map/ppermute | solution.py:504
  5.9 0.5 collective-permute-start.1
  6.5 0.1 collective-permute-start
  6.6 1.9 %collective-permute-done.2.refs_3_ = bf16[104,384]{1,0:T(8,128)(2,1)S(1)} collective-permute-done((bf16[104,384]{1,0:T(8,128)(2,1)S(1)}, bf16[104,384]{1,0:T(8,128)(2,1)S(1)}, u32[]{:S(2)}, u32[]{:S(2)}) %collective-permute-start.2) | collective-permute-done | bytes 79904 | tf_op jit(solution)/shard_map/ppermute | solution.py:504
  8.5 1.9 %collective-permute-done.1.refs_2_ = bf16[104,384]{1,0:T(8,128)(2,1)S(1)} collective-permute-done((bf16[104,384]{1,0:T(8,128)(2,1)S(1)}, bf16[104,384]{1,0:T(8,128)(2,1)S(1)}, u32[]{:S(2)}, u32[]{:S(2)}) %collective-permute-start.1) | collective-permute-done | bytes 79904 | tf_op jit(solution)/shard_map/ppermute | solution.py:504
  10.4 0.5 collective-permute-done.refs_1_
  10.9 1.7 %rotor.1 = (bf16[96,384]{1,0:T(8,128)(2,1)S(1)}, bf16[24,384]{1,0:T(8,128)(2,1)S(1)}, bf16[544,384]{1,0:T(8,128)(2,1)S(1)}, bf16[128,384]{1,0:T(8,128)(2,1)S(1)}) custom-call(bf16[104,384]{1,0:T(8,128)(2,1)S(1)} %gram.1.refs_0_, bf16[104,384]{1,0:T(8,128)(2,1)S(1)} %collective-permute-done.refs_1_, bf16[104,384]{1,0:T(8,128)(2,1)S(1)} %collective-permute-done.1.refs_2_, ...), custom_call_target="tpu_custom_call" | custom-call | flops 264241152 | bytes 1548288 | tf_op jit(solution)/shard_map/rotor/pallas_call | solution.py:318
  12.6 1.6 %collective-permute-start.3 = (bf16[544,384]{1,0:T(8,128)(2,1)S(1)}, bf16[544,384]{1,0:T(8,128)(2,1)S(1)}, u32[]{:S(2)}, u32[]{:S(2)}) collective-permute-start(bf16[544,384]{1,0:T(8,128)(2,1)S(1)} %get-tuple-element.17.refs_0_), channel_id=1, source_target_pairs={{0,2},{1,3},{2,4},{3,5},{4,6},{5,7},{6,0},{7,1},{8,10},{9,11},{10,... | collective-permute-start | bytes 1253384 | tf_op jit(solution)/shard_map/ppermute | solution.py:497
  14.3 1.1 %taken.1 = bf16[704,384]{1,0:T(8,128)(2,1)S(1)} custom-call(bf16[2048,384]{1,0:T(8,128)(2,1)} %x_hbm.1), custom_call_target="tpu_custom_call" | custom-call | bytes 1081344 | tf_op jit(solution)/shard_map/taken/pallas_call | solution.py:113
  15.3 1.6 %collective-permute-start.9 = (bf16[704,384]{1,0:T(8,128)(2,1)S(1)}, bf16[704,384]{1,0:T(8,128)(2,1)S(1)}, u32[]{:S(2)}, u32[]{:S(2)}) collective-permute-start(bf16[704,384]{1,0:T(8,128)(2,1)S(1)} %taken.1), channel_id=1, source_target_pairs={{0,2},{1,3},{2,4},{3,5},{4,6},{5,7},{6,0},{7,1},{8,10},{9,11},{10,... | collective-permute-start | bytes 1622024 | tf_op jit(solution)/shard_map/ppermute | solution.py:497
  16.9 0.0 copy-done.1
  16.9 1.6 %rotate.1 = (bf16[704,384]{1,0:T(8,128)(2,1)S(1)}, bf16[320,384]{1,0:T(8,128)(2,1)S(1)}) custom-call(bf16[96,384]{1,0:T(8,128)(2,1)S(1)} %get-tuple-element.19.refs_0_.s_ref, bf16[2048,384]{1,0:T(8,128)(2,1)S(1)} %copy-done.1), custom_call_target="tpu_custom_call" | custom-call | flops 402653184 | bytes 2359296 | tf_op jit(solution)/shard_map/rotate/pallas_call | solution.py:358
  18.5 8.6 %collective-permute-done.3.refs_0_ = bf16[544,384]{1,0:T(8,128)(2,1)S(1)} collective-permute-done((bf16[544,384]{1,0:T(8,128)(2,1)S(1)}, bf16[544,384]{1,0:T(8,128)(2,1)S(1)}, u32[]{:S(2)}, u32[]{:S(2)}) %collective-permute-start.3) | collective-permute-done | bytes 417824 | tf_op jit(solution)/shard_map/ppermute | solution.py:497
  27.2 1.6 %collective-permute-start.15 = (bf16[704,384]{1,0:T(8,128)(2,1)S(1)}, bf16[704,384]{1,0:T(8,128)(2,1)S(1)}, u32[]{:S(2)}, u32[]{:S(2)}) collective-permute-start(bf16[704,384]{1,0:T(8,128)(2,1)S(1)} %get-tuple-element.28.refs_3_), channel_id=1, source_target_pairs={{0,6},{1,7},{2,0},{3,1},{4,2},{5,3},{6,4},{7,5},{8,14},{9,15},{10,... | collective-permute-start | bytes 1622024 | tf_op jit(solution)/shard_map/ppermute | solution.py:497
  28.8 0.4 collective-permute-start.4
  29.2 0.0 collective-permute-start.5
  29.2 21.7 %collective-permute-done.5.refs_0_ = bf16[24,384]{1,0:T(8,128)(2,1)S(1)} collective-permute-done((bf16[24,384]{1,0:T(8,128)(2,1)S(1)}, bf16[24,384]{1,0:T(8,128)(2,1)S(1)}, u32[]{:S(2)}, u32[]{:S(2)}) %collective-permute-start.5) | collective-permute-done | bytes 18464 | tf_op jit(solution)/shard_map/ppermute | solution.py:497
  50.9 1.3 %collective-permute-start.8 = (bf16[24,384]{1,0:T(8,128)(2,1)S(1)}, bf16[24,384]{1,0:T(8,128)(2,1)S(1)}, u32[]{:S(2)}, u32[]{:S(2)}) collective-permute-start(bf16[24,384]{1,0:T(8,128)(2,1)S(1)} %collective-permute-done.5.refs_0_), channel_id=1, source_target_pairs={{0,24},{8,16},{16,8},{24,0},{1,25},{9,17},{17,9},{25,1},{2,26},{10... | collective-permute-start | bytes 55304 | tf_op jit(solution)/shard_map/ppermute | solution.py:504
  52.3 1.7 %collective-permute-start.7 = (bf16[24,384]{1,0:T(8,128)(2,1)S(1)}, bf16[24,384]{1,0:T(8,128)(2,1)S(1)}, u32[]{:S(2)}, u32[]{:S(2)}) collective-permute-start(bf16[24,384]{1,0:T(8,128)(2,1)S(1)} %collective-permute-done.5.refs_0_), channel_id=1, source_target_pairs={{0,16},{8,24},{16,0},{24,8},{1,17},{9,25},{17,1},{25,9},{2,18},{10... | collective-permute-start | bytes 55304 | tf_op jit(solution)/shard_map/ppermute | solution.py:504
  53.9 1.7 %collective-permute-done.8.refs_3_ = bf16[24,384]{1,0:T(8,128)(2,1)S(1)} collective-permute-done((bf16[24,384]{1,0:T(8,128)(2,1)S(1)}, bf16[24,384]{1,0:T(8,128)(2,1)S(1)}, u32[]{:S(2)}, u32[]{:S(2)}) %collective-permute-start.8) | collective-permute-done | bytes 18464 | tf_op jit(solution)/shard_map/ppermute | solution.py:504
  55.6 1.5 %collective-permute-start.6 = (bf16[24,384]{1,0:T(8,128)(2,1)S(1)}, bf16[24,384]{1,0:T(8,128)(2,1)S(1)}, u32[]{:S(2)}, u32[]{:S(2)}) collective-permute-start(bf16[24,384]{1,0:T(8,128)(2,1)S(1)} %collective-permute-done.5.refs_0_), channel_id=1, source_target_pairs={{0,8},{8,0},{16,24},{24,16},{1,9},{9,1},{17,25},{25,17},{2,10},{10... | collective-permute-start | bytes 55304 | tf_op jit(solution)/shard_map/ppermute | solution.py:504
  57.1 0.0 collective-permute-done.7.refs_2_
  57.1 2.2 %collective-permute-done.6.refs_1_ = bf16[24,384]{1,0:T(8,128)(2,1)S(1)} collective-permute-done((bf16[24,384]{1,0:T(8,128)(2,1)S(1)}, bf16[24,384]{1,0:T(8,128)(2,1)S(1)}, u32[]{:S(2)}, u32[]{:S(2)}) %collective-permute-start.6) | collective-permute-done | bytes 18464 | tf_op jit(solution)/shard_map/ppermute | solution.py:504
  59.4 0.0 collective-permute-done.9.refs_4_
  59.4 1.3 %tail.3.refs_2_ = bf16[352,384]{1,0:T(8,128)(2,1)S(1)} custom-call(bf16[24,384]{1,0:T(8,128)(2,1)S(1)} %collective-permute-done.5.refs_0_, bf16[24,384]{1,0:T(8,128)(2,1)S(1)} %collective-permute-done.6.refs_1_, bf16[24,384]{1,0:T(8,128)(2,1)S(1)} %collective-permute-done.7.refs_2_, bf16[24,384]{1,0:T(8,128)(2,1)S(1)} %collective-permute-done.8.refs_3_, ...), custom_call_target="tpu_custom_call" | custom-call | flops 138412032 | bytes 811008 | tf_op jit(solution)/shard_map/tail/pallas_call | solution.py:338
  60.6 0.0 collective-permute-done.4.refs_1_
  60.6 0.8 gram_pair.1.refs_0_
  61.4 1.4 %collective-permute-start.12 = (bf16[104,384]{1,0:T(8,128)(2,1)S(1)}, bf16[104,384]{1,0:T(8,128)(2,1)S(1)}, u32[]{:S(2)}, u32[]{:S(2)}) collective-permute-start(bf16[104,384]{1,0:T(8,128)(2,1)S(1)} %gram_pair.1.refs_0_), channel_id=1, source_target_pairs={{0,24},{8,16},{16,8},{24,0},{1,25},{9,17},{17,9},{25,1},{2,26},{10... | collective-permute-start | bytes 239624 | tf_op jit(solution)/shard_map/ppermute | solution.py:504
  62.8 1.7 %collective-permute-start.11 = (bf16[104,384]{1,0:T(8,128)(2,1)S(1)}, bf16[104,384]{1,0:T(8,128)(2,1)S(1)}, u32[]{:S(2)}, u32[]{:S(2)}) collective-permute-start(bf16[104,384]{1,0:T(8,128)(2,1)S(1)} %gram_pair.1.refs_0_), channel_id=1, source_target_pairs={{0,16},{8,24},{16,0},{24,8},{1,17},{9,25},{17,1},{25,9},{2,18},{10... | collective-permute-start | bytes 239624 | tf_op jit(solution)/shard_map/ppermute | solution.py:504
  64.5 0.5 collective-permute-start.10
  65.0 1.9 %collective-permute-done.12.refs_3_ = bf16[104,384]{1,0:T(8,128)(2,1)S(1)} collective-permute-done((bf16[104,384]{1,0:T(8,128)(2,1)S(1)}, bf16[104,384]{1,0:T(8,128)(2,1)S(1)}, u32[]{:S(2)}, u32[]{:S(2)}) %collective-permute-start.12) | collective-permute-done | bytes 79904 | tf_op jit(solution)/shard_map/ppermute | solution.py:504
  66.9 0.8 %collective-permute-done.11.refs_2_ = bf16[104,384]{1,0:T(8,128)(2,1)S(1)} collective-permute-done((bf16[104,384]{1,0:T(8,128)(2,1)S(1)}, bf16[104,384]{1,0:T(8,128)(2,1)S(1)}, u32[]{:S(2)}, u32[]{:S(2)}) %collective-permute-start.11) | collective-permute-done | bytes 79904 | tf_op jit(solution)/shard_map/ppermute | solution.py:504
  67.7 1.2 %collective-permute-done.10.refs_1_ = bf16[104,384]{1,0:T(8,128)(2,1)S(1)} collective-permute-done((bf16[104,384]{1,0:T(8,128)(2,1)S(1)}, bf16[104,384]{1,0:T(8,128)(2,1)S(1)}, u32[]{:S(2)}, u32[]{:S(2)}) %collective-permute-start.10) | collective-permute-done | bytes 79904 | tf_op jit(solution)/shard_map/ppermute | solution.py:504
  68.9 1.2 %second.1 = (bf16[96,384]{1,0:T(8,128)(2,1)S(1)}, bf16[384,256]{1,0:T(8,128)(2,1)S(1)}) custom-call(bf16[104,384]{1,0:T(8,128)(2,1)S(1)} %gram_pair.1.refs_0_, bf16[104,384]{1,0:T(8,128)(2,1)S(1)} %collective-permute-done.10.refs_1_, bf16[104,384]{1,0:T(8,128)(2,1)S(1)} %collective-permute-done.11.refs_2_, bf16[104,384]{1,0:T(8,128)(2,1)S(1)} %collective-permute-done.12.refs_3_), custom_call_target="tpu_custom_call" | custom-call | flops 134217728 | bytes 262144 | tf_op jit(solution)/shard_map/second/pallas_call | solution.py:380
  70.1 1.7 %collective-permute-start.13 = (bf16[320,384]{1,0:T(8,128)(2,1)S(1)}, bf16[320,384]{1,0:T(8,128)(2,1)S(1)}, u32[]{:S(2)}, u32[]{:S(2)}) collective-permute-start(bf16[320,384]{1,0:T(8,128)(2,1)S(1)} %get-tuple-element.25.refs_4_), channel_id=1, source_target_pairs={{0,6},{1,7},{2,0},{3,1},{4,2},{5,3},{6,4},{7,5},{8,14},{9,15},{10,... | collective-permute-start | bytes 737288 | tf_op jit(solution)/shard_map/ppermute | solution.py:497
  71.8 0.4 collective-permute-start.14
  72.3 1.3 %tail.2.refs_2_ = bf16[352,384]{1,0:T(8,128)(2,1)S(1)} custom-call(bf16[96,384]{1,0:T(8,128)(2,1)S(1)} %get-tuple-element.19.refs_0_.s_ref, bf16[2048,384]{1,0:T(8,128)(2,1)S(1)} %copy-done.1), custom_call_target="tpu_custom_call" | custom-call | flops 138412032 | bytes 811008 | tf_op jit(solution)/shard_map/tail/pallas_call | solution.py:338
  73.6 0.8 left_half.1.refs_4_
  74.3 2.9 %collective-permute-done.14.s_ref = bf16[96,384]{1,0:T(8,128)(2,1)S(1)} collective-permute-done((bf16[96,384]{1,0:T(8,128)(2,1)S(1)}, bf16[96,384]{1,0:T(8,128)(2,1)S(1)}, u32[]{:S(2)}, u32[]{:S(2)}) %collective-permute-start.14) | collective-permute-done | bytes 73760 | tf_op jit(solution)/shard_map/ppermute | solution.py:497
  77.2 0.9 %right.1.refs_5_ = bf16[384,256]{1,0:T(8,128)(2,1)S(1)} custom-call(bf16[96,384]{1,0:T(8,128)(2,1)S(1)} %collective-permute-done.14.s_ref), custom_call_target="tpu_custom_call" | custom-call | flops 134217728 | bytes 262144 | tf_op jit(solution)/shard_map/right/pallas_call | solution.py:398
  78.0 0.0 collective-permute-done.15.refs_3_
  78.1 1.5 %final.2.refs_6_ = bf16[2048,384]{1,0:T(8,128)(2,1)} custom-call(bf16[544,384]{1,0:T(8,128)(2,1)S(1)} %get-tuple-element.17.refs_0_, bf16[128,384]{1,0:T(8,128)(2,1)S(1)} %get-tuple-element.18.refs_1_, bf16[352,384]{1,0:T(8,128)(2,1)S(1)} %tail.2.refs_2_, bf16[704,384]{1,0:T(8,128)(2,1)S(1)} %collective-permute-done.15.refs_3_, ...), custom_call_target="tpu_custom_call" | custom-call | flops 369098752 | bytes 2162688 | tf_op jit(solution)/shard_map/final/pallas_call | solution.py:479
  79.5 0.0 collective-permute-done.13.refs_3_
  79.6 1.1 %final.3 = bf16[2048,384]{1,0:T(8,128)(2,1)} custom-call(bf16[544,384]{1,0:T(8,128)(2,1)S(1)} %get-tuple-element.17.refs_0_, bf16[128,384]{1,0:T(8,128)(2,1)S(1)} %get-tuple-element.18.refs_1_, bf16[352,384]{1,0:T(8,128)(2,1)S(1)} %tail.2.refs_2_, bf16[320,384]{1,0:T(8,128)(2,1)S(1)} %collective-permute-done.13.refs_3_, ...), custom_call_target="tpu_custom_call", output_to_operand_aliasing={{}: (6, {})} | custom-call | flops 167772160 | bytes 983040 | tf_op jit(solution)/shard_map/final/pallas_call | solution.py:479
Async XLA Ops:
  0.0 1.4 %copy-start = (bf16[2048,384]{1,0:T(8,128)(2,1)S(1)}, bf16[2048,384]{1,0:T(8,128)(2,1)}, u32[]{:S(2)}) copy-start(bf16[2048,384]{1,0:T(8,128)(2,1)} %x_hbm.1) | copy-start | bytes 4718596
  1.9 15.0 %copy-start.1 = (bf16[2048,384]{1,0:T(8,128)(2,1)S(1)}, bf16[2048,384]{1,0:T(8,128)(2,1)}, u32[]{:S(2)}) copy-start(bf16[2048,384]{1,0:T(8,128)(2,1)} %x_hbm.1) | copy-start | bytes 4718596
  2.0 6.5 %collective-permute-start.2 = (bf16[104,384]{1,0:T(8,128)(2,1)S(1)}, bf16[104,384]{1,0:T(8,128)(2,1)S(1)}, u32[]{:S(2)}, u32[]{:S(2)}) collective-permute-start(bf16[104,384]{1,0:T(8,128)(2,1)S(1)} %gram.1.refs_0_), channel_id=1, source_target_pairs={{0,24},{8,16},{16,8},{24,0},{1,25},{9,17},{17,9},{25,1},{2,26},{10... | collective-permute-start | bytes 239624 | tf_op jit(solution)/shard_map/ppermute | solution.py:504
  5.9 4.4 %collective-permute-start.1 = (bf16[104,384]{1,0:T(8,128)(2,1)S(1)}, bf16[104,384]{1,0:T(8,128)(2,1)S(1)}, u32[]{:S(2)}, u32[]{:S(2)}) collective-permute-start(bf16[104,384]{1,0:T(8,128)(2,1)S(1)} %gram.1.refs_0_), channel_id=1, source_target_pairs={{0,16},{8,24},{16,0},{24,8},{1,17},{9,25},{17,1},{25,9},{2,18},{10... | collective-permute-start | bytes 239624 | tf_op jit(solution)/shard_map/ppermute | solution.py:504
  6.5 4.4 %collective-permute-start = (bf16[104,384]{1,0:T(8,128)(2,1)S(1)}, bf16[104,384]{1,0:T(8,128)(2,1)S(1)}, u32[]{:S(2)}, u32[]{:S(2)}) collective-permute-start(bf16[104,384]{1,0:T(8,128)(2,1)S(1)} %gram.1.refs_0_), channel_id=1, source_target_pairs={{0,8},{8,0},{16,24},{24,16},{1,9},{9,1},{17,25},{25,17},{2,10},{10... | collective-permute-start | bytes 239624 | tf_op jit(solution)/shard_map/ppermute | solution.py:504
  12.6 14.6 %collective-permute-start.3 = (bf16[544,384]{1,0:T(8,128)(2,1)S(1)}, bf16[544,384]{1,0:T(8,128)(2,1)S(1)}, u32[]{:S(2)}, u32[]{:S(2)}) collective-permute-start(bf16[544,384]{1,0:T(8,128)(2,1)S(1)} %get-tuple-element.17.refs_0_), channel_id=1, source_target_pairs={{0,2},{1,3},{2,4},{3,5},{4,6},{5,7},{6,0},{7,1},{8,10},{9,11},{10,... | collective-permute-start | bytes 1253384 | tf_op jit(solution)/shard_map/ppermute | solution.py:497
  15.3 44.0 %collective-permute-start.9 = (bf16[704,384]{1,0:T(8,128)(2,1)S(1)}, bf16[704,384]{1,0:T(8,128)(2,1)S(1)}, u32[]{:S(2)}, u32[]{:S(2)}) collective-permute-start(bf16[704,384]{1,0:T(8,128)(2,1)S(1)} %taken.1), channel_id=1, source_target_pairs={{0,2},{1,3},{2,4},{3,5},{4,6},{5,7},{6,0},{7,1},{8,10},{9,11},{10,... | collective-permute-start | bytes 1622024 | tf_op jit(solution)/shard_map/ppermute | solution.py:497
  27.2 50.9 %collective-permute-start.15 = (bf16[704,384]{1,0:T(8,128)(2,1)S(1)}, bf16[704,384]{1,0:T(8,128)(2,1)S(1)}, u32[]{:S(2)}, u32[]{:S(2)}) collective-permute-start(bf16[704,384]{1,0:T(8,128)(2,1)S(1)} %get-tuple-element.28.refs_3_), channel_id=1, source_target_pairs={{0,6},{1,7},{2,0},{3,1},{4,2},{5,3},{6,4},{7,5},{8,14},{9,15},{10,... | collective-permute-start | bytes 1622024 | tf_op jit(solution)/shard_map/ppermute | solution.py:497
  28.8 31.8 %collective-permute-start.4 = (bf16[128,384]{1,0:T(8,128)(2,1)S(1)}, bf16[128,384]{1,0:T(8,128)(2,1)S(1)}, u32[]{:S(2)}, u32[]{:S(2)}) collective-permute-start(bf16[128,384]{1,0:T(8,128)(2,1)S(1)} %get-tuple-element.18.refs_1_), channel_id=1, source_target_pairs={{0,2},{1,3},{2,4},{3,5},{4,6},{5,7},{6,0},{7,1},{8,10},{9,11},{10,... | collective-permute-start | bytes 294920 | tf_op jit(solution)/shard_map/ppermute | solution.py:497
  29.2 21.7 %collective-permute-start.5 = (bf16[24,384]{1,0:T(8,128)(2,1)S(1)}, bf16[24,384]{1,0:T(8,128)(2,1)S(1)}, u32[]{:S(2)}, u32[]{:S(2)}) collective-permute-start(bf16[24,384]{1,0:T(8,128)(2,1)S(1)} %get-tuple-element.22), channel_id=1, source_target_pairs={{0,2},{1,3},{2,4},{3,5},{4,6},{5,7},{6,0},{7,1},{8,10},{9,11},{10,... | collective-permute-start | bytes 55304 | tf_op jit(solution)/shard_map/ppermute | solution.py:497
  50.9 4.7 %collective-permute-start.8 = (bf16[24,384]{1,0:T(8,128)(2,1)S(1)}, bf16[24,384]{1,0:T(8,128)(2,1)S(1)}, u32[]{:S(2)}, u32[]{:S(2)}) collective-permute-start(bf16[24,384]{1,0:T(8,128)(2,1)S(1)} %collective-permute-done.5.refs_0_), channel_id=1, source_target_pairs={{0,24},{8,16},{16,8},{24,0},{1,25},{9,17},{17,9},{25,1},{2,26},{10... | collective-permute-start | bytes 55304 | tf_op jit(solution)/shard_map/ppermute | solution.py:504
  52.3 4.9 %collective-permute-start.7 = (bf16[24,384]{1,0:T(8,128)(2,1)S(1)}, bf16[24,384]{1,0:T(8,128)(2,1)S(1)}, u32[]{:S(2)}, u32[]{:S(2)}) collective-permute-start(bf16[24,384]{1,0:T(8,128)(2,1)S(1)} %collective-permute-done.5.refs_0_), channel_id=1, source_target_pairs={{0,16},{8,24},{16,0},{24,8},{1,17},{9,25},{17,1},{25,9},{2,18},{10... | collective-permute-start | bytes 55304 | tf_op jit(solution)/shard_map/ppermute | solution.py:504
  55.6 3.8 %collective-permute-start.6 = (bf16[24,384]{1,0:T(8,128)(2,1)S(1)}, bf16[24,384]{1,0:T(8,128)(2,1)S(1)}, u32[]{:S(2)}, u32[]{:S(2)}) collective-permute-start(bf16[24,384]{1,0:T(8,128)(2,1)S(1)} %collective-permute-done.5.refs_0_), channel_id=1, source_target_pairs={{0,8},{8,0},{16,24},{24,16},{1,9},{9,1},{17,25},{25,17},{2,10},{10... | collective-permute-start | bytes 55304 | tf_op jit(solution)/shard_map/ppermute | solution.py:504
  61.4 5.4 %collective-permute-start.12 = (bf16[104,384]{1,0:T(8,128)(2,1)S(1)}, bf16[104,384]{1,0:T(8,128)(2,1)S(1)}, u32[]{:S(2)}, u32[]{:S(2)}) collective-permute-start(bf16[104,384]{1,0:T(8,128)(2,1)S(1)} %gram_pair.1.refs_0_), channel_id=1, source_target_pairs={{0,24},{8,16},{16,8},{24,0},{1,25},{9,17},{17,9},{25,1},{2,26},{10... | collective-permute-start | bytes 239624 | tf_op jit(solution)/shard_map/ppermute | solution.py:504
  62.8 4.8 %collective-permute-start.11 = (bf16[104,384]{1,0:T(8,128)(2,1)S(1)}, bf16[104,384]{1,0:T(8,128)(2,1)S(1)}, u32[]{:S(2)}, u32[]{:S(2)}) collective-permute-start(bf16[104,384]{1,0:T(8,128)(2,1)S(1)} %gram_pair.1.refs_0_), channel_id=1, source_target_pairs={{0,16},{8,24},{16,0},{24,8},{1,17},{9,25},{17,1},{25,9},{2,18},{10... | collective-permute-start | bytes 239624 | tf_op jit(solution)/shard_map/ppermute | solution.py:504
  64.5 4.4 %collective-permute-start.10 = (bf16[104,384]{1,0:T(8,128)(2,1)S(1)}, bf16[104,384]{1,0:T(8,128)(2,1)S(1)}, u32[]{:S(2)}, u32[]{:S(2)}) collective-permute-start(bf16[104,384]{1,0:T(8,128)(2,1)S(1)} %gram_pair.1.refs_0_), channel_id=1, source_target_pairs={{0,8},{8,0},{16,24},{24,16},{1,9},{9,1},{17,25},{25,17},{2,10},{10... | collective-permute-start | bytes 239624 | tf_op jit(solution)/shard_map/ppermute | solution.py:504
  70.1 9.4 %collective-permute-start.13 = (bf16[320,384]{1,0:T(8,128)(2,1)S(1)}, bf16[320,384]{1,0:T(8,128)(2,1)S(1)}, u32[]{:S(2)}, u32[]{:S(2)}) collective-permute-start(bf16[320,384]{1,0:T(8,128)(2,1)S(1)} %get-tuple-element.25.refs_4_), channel_id=1, source_target_pairs={{0,6},{1,7},{2,0},{3,1},{4,2},{5,3},{6,4},{7,5},{8,14},{9,15},{10,... | collective-permute-start | bytes 737288 | tf_op jit(solution)/shard_map/ppermute | solution.py:497
  71.8 5.3 %collective-permute-start.14 = (bf16[96,384]{1,0:T(8,128)(2,1)S(1)}, bf16[96,384]{1,0:T(8,128)(2,1)S(1)}, u32[]{:S(2)}, u32[]{:S(2)}) collective-permute-start(bf16[96,384]{1,0:T(8,128)(2,1)S(1)} %get-tuple-element.27), channel_id=1, source_target_pairs={{0,6},{1,7},{2,0},{3,1},{4,2},{5,3},{6,4},{7,5},{8,14},{9,15},{10,... | collective-permute-start | bytes 221192 | tf_op jit(solution)/shard_map/ppermute | solution.py:497

commit v4 on v3

--- a/solution.py
+++ b/solution.py
@@ -89,7 +89,8 @@
     h = half // 2
     packed_store(g_ref, slice(0, h), *pack_window(cross[:h], cross[h:], half), half)
     row = lax.broadcasted_iota(jnp.int32, (8, g_ref.shape[1]), 0)
-    g_ref[h:] = low(jnp.where(row == 0, norms, 0.0))
+    rest = norms - low(norms).astype(F32)
+    g_ref[h:] = low(jnp.where(row == 0, norms, jnp.where(row == 1, rest, 0.0)))
 
 
 def stats_shape(cols):
@@ -194,7 +195,7 @@
     w = window(half)
     pad, h = w - half, half // 2
     cross = unpack_window(total[:h])
-    norms = total[h:]
+    norms = total[h:] + pltpu.roll(total[h:], 7, 0)
     left = jnp.transpose(norms[:, :w])[:half, :1]
     corr = cross * (lax.rsqrt(left) * lax.rsqrt(norms[:1, cols - w :]))
     lane = lax.broadcasted_iota(jnp.int32, corr.shape, 1)
@@ -208,8 +209,24 @@
     return jnp.concatenate([x, jnp.zeros((w - half, w), F32)], axis=0) if w > half else x
 
 
-def minus_constant(k, k2):
-    return COEF[1] * k + COEF[2] * k2 + dot(low(k2), low(COEF[3] * k + COEF[4] * k2), (1, 0))
+def split(a):
+    high = low(a)
+    return high, low(a - high.astype(F32))
+
+
+def split_dot(a, b, contract=(1, 0)):
+    return dot(a[0], b[0], contract) + (dot(a[0], b[1], contract) + dot(a[1], b[0], contract))
+
+
+def minus_constant(k):
+    words = split(k)
+    k2 = split_dot(words, words)
+    return COEF[1] * k + COEF[2] * k2 + split_dot(split(k2), split(COEF[3] * k + COEF[4] * k2))
+
+
+def word_dot(x, delta, contract):
+    high, rest = split(delta)
+    return dot(x, high, contract) + dot(x, rest, contract)
 
 
 def eye_at(w, first, stop):
@@ -222,9 +239,9 @@
     w = x.shape[1]
     xb = low(x)
     k = dot(xb, xb, (1, 1))
-    delta = minus_constant(k, dot(low(k), low(k), (1, 0)))
+    delta = minus_constant(k)
     upper = delta + jnp.where(eye_at(w, 0, half), COEF[0], 0.0)
-    lower = -(COEF[0] * jnp.transpose(x) + dot(xb, low(delta), (0, 0)))
+    lower = -(COEF[0] * jnp.transpose(x) + word_dot(xb, delta, (0, 0)))
     return low(jnp.concatenate([upper[:half], lower[w - half :]], axis=0))
 
 
@@ -232,8 +249,8 @@
     w = x.shape[1]
     xb = low(x)
     k = dot(xb, xb, (0, 0))
-    delta = minus_constant(k, dot(low(k), low(k), (1, 0)))
-    upper = COEF[0] * x + dot(xb, low(delta), (1, 0))
+    delta = minus_constant(k)
+    upper = COEF[0] * x + word_dot(xb, delta, (1, 0))
     lower = delta + jnp.where(eye_at(w, w - half, w), COEF[0], 0.0)
     return low(jnp.concatenate([upper[:half], lower[w - half :]], axis=0))
 

time: 80.8 us -> 82.2 us (1.017)
  Pallas kernels: 13.7 us -> 15.9 us
  transfers between devices with their start and end apart: 16 -> 16, of which waited for: 11 -> 11; matrix products, arithmetic and copies ran while one was open for 0% -> 0% of each run, Pallas kernels for 13% -> 15%
where the time goes in v4:
time: 82.2 us; the launch traced here: 82.1 us
  waiting for transfers between devices  44.6 us (54%)
  starting transfers between devices  20.1 us (24%)
  Pallas kernels  15.9 us (19%)
  local copies, waits for them, and re-layouts  1.41 us (2%)
    ppermute x7, waiting for transfers between devices, passed(): return lax.ppermute(x, 'pairs', [(i, (i + 2 * by) % n) for i in range(n)])  32.4 us
    ppermute x9, starting transfers between devices, row_parts(): lax.ppermute(g, 'rows', [(i, i ^ k) for i in range(n)])  12.7 us
    ppermute x9, waiting for transfers between devices, row_parts(): lax.ppermute(g, 'rows', [(i, i ^ k) for i in range(n)])  12.1 us
    ppermute x7, starting transfers between devices, passed(): return lax.ppermute(x, 'pairs', [(i, (i + 2 * by) % n) for i in range(n)])  7.46 us
    pallas_call x2, Pallas kernels, tail(): pl.pallas_call(tail_kernel, in_specs=whole(len(s) + 1), out_specs=whole(1...  3.22 us
    pallas_call x2, Pallas kernels, final(): pl.pallas_call(functools.partial(final_kernel, base, cuts, len(a)), in_sp...  2.62 us
    pallas_call x1, Pallas kernels, rotor(): pl.pallas_call(functools.partial(rotor_kernel, len(parts)), in_specs=whol...  2.09 us
    pallas_call x1, Pallas kernels, rotate(): pl.pallas_call(rotate_kernel, in_specs=whole(2), out_specs=whole(len(size...  1.99 us
  transfers between devices with their start and end apart: 16, of which 11 were waited for; matrix products, arithmetic and copies ran while one was open for 0% of the time, Pallas kernels for 15%

profile of v4, /device:TPU:0, one launch (start us, length us, event | category | flops | bytes accessed | tf_op | source)
XLA Modules:
  0.0 82.1 jit_solution(14561623991247749859)
XLA Ops:
  0.0 0.0 copy-start
  0.0 1.4 %copy-done = bf16[2048,384]{1,0:T(8,128)(2,1)S(1)} copy-done((bf16[2048,384]{1,0:T(8,128)(2,1)S(1)}, bf16[2048,384]{1,0:T(8,128)(2,1)}, u32[]{:S(2)}) %copy-start) | copy-done | bytes 1572888
  1.4 0.5 gram.1.refs_0_
  1.9 0.0 copy-start.1
  2.0 4.0 %collective-permute-start.2 = (bf16[104,384]{1,0:T(8,128)(2,1)S(1)}, bf16[104,384]{1,0:T(8,128)(2,1)S(1)}, u32[]{:S(2)}, u32[]{:S(2)}) collective-permute-start(bf16[104,384]{1,0:T(8,128)(2,1)S(1)} %gram.1.refs_0_), channel_id=1, source_target_pairs={{0,24},{8,16},{16,8},{24,0},{1,25},{9,17},{17,9},{25,1},{2,26},{10... | collective-permute-start | bytes 239624 | tf_op jit(solution)/shard_map/ppermute | solution.py:521
  5.9 0.5 collective-permute-start.1
  6.5 0.1 collective-permute-start
  6.6 1.9 %collective-permute-done.2.refs_3_ = bf16[104,384]{1,0:T(8,128)(2,1)S(1)} collective-permute-done((bf16[104,384]{1,0:T(8,128)(2,1)S(1)}, bf16[104,384]{1,0:T(8,128)(2,1)S(1)}, u32[]{:S(2)}, u32[]{:S(2)}) %collective-permute-start.2) | collective-permute-done | bytes 79904 | tf_op jit(solution)/shard_map/ppermute | solution.py:521
  8.5 1.9 %collective-permute-done.1.refs_2_ = bf16[104,384]{1,0:T(8,128)(2,1)S(1)} collective-permute-done((bf16[104,384]{1,0:T(8,128)(2,1)S(1)}, bf16[104,384]{1,0:T(8,128)(2,1)S(1)}, u32[]{:S(2)}, u32[]{:S(2)}) %collective-permute-start.1) | collective-permute-done | bytes 79904 | tf_op jit(solution)/shard_map/ppermute | solution.py:521
  10.4 0.5 collective-permute-done.refs_1_
  10.9 2.1 %rotor.1 = (bf16[96,384]{1,0:T(8,128)(2,1)S(1)}, bf16[24,384]{1,0:T(8,128)(2,1)S(1)}, bf16[544,384]{1,0:T(8,128)(2,1)S(1)}, bf16[128,384]{1,0:T(8,128)(2,1)S(1)}) custom-call(bf16[104,384]{1,0:T(8,128)(2,1)S(1)} %gram.1.refs_0_, bf16[104,384]{1,0:T(8,128)(2,1)S(1)} %collective-permute-done.refs_1_, bf16[104,384]{1,0:T(8,128)(2,1)S(1)} %collective-permute-done.1.refs_2_, ...), custom_call_target="tpu_custom_call" | custom-call | flops 264241152 | bytes 1548288 | tf_op jit(solution)/shard_map/rotor/pallas_call | solution.py:335
  13.0 1.6 %collective-permute-start.3 = (bf16[544,384]{1,0:T(8,128)(2,1)S(1)}, bf16[544,384]{1,0:T(8,128)(2,1)S(1)}, u32[]{:S(2)}, u32[]{:S(2)}) collective-permute-start(bf16[544,384]{1,0:T(8,128)(2,1)S(1)} %get-tuple-element.17.refs_0_), channel_id=1, source_target_pairs={{0,2},{1,3},{2,4},{3,5},{4,6},{5,7},{6,0},{7,1},{8,10},{9,11},{10,... | collective-permute-start | bytes 1253384 | tf_op jit(solution)/shard_map/ppermute | solution.py:514
  14.6 1.1 %taken.1 = bf16[704,384]{1,0:T(8,128)(2,1)S(1)} custom-call(bf16[2048,384]{1,0:T(8,128)(2,1)} %x_hbm.1), custom_call_target="tpu_custom_call" | custom-call | bytes 1081344 | tf_op jit(solution)/shard_map/taken/pallas_call | solution.py:114
  15.7 1.6 %collective-permute-start.9 = (bf16[704,384]{1,0:T(8,128)(2,1)S(1)}, bf16[704,384]{1,0:T(8,128)(2,1)S(1)}, u32[]{:S(2)}, u32[]{:S(2)}) collective-permute-start(bf16[704,384]{1,0:T(8,128)(2,1)S(1)} %taken.1), channel_id=1, source_target_pairs={{0,2},{1,3},{2,4},{3,5},{4,6},{5,7},{6,0},{7,1},{8,10},{9,11},{10,... | collective-permute-start | bytes 1622024 | tf_op jit(solution)/shard_map/ppermute | solution.py:514
  17.3 0.0 copy-done.1
  17.3 2.0 %rotate.1 = (bf16[704,384]{1,0:T(8,128)(2,1)S(1)}, bf16[320,384]{1,0:T(8,128)(2,1)S(1)}) custom-call(bf16[96,384]{1,0:T(8,128)(2,1)S(1)} %get-tuple-element.19.refs_0_.s_ref, bf16[2048,384]{1,0:T(8,128)(2,1)S(1)} %copy-done.1), custom_call_target="tpu_custom_call" | custom-call | flops 402653184 | bytes 2359296 | tf_op jit(solution)/shard_map/rotate/pallas_call | solution.py:375
  19.3 8.2 %collective-permute-done.3.refs_0_ = bf16[544,384]{1,0:T(8,128)(2,1)S(1)} collective-permute-done((bf16[544,384]{1,0:T(8,128)(2,1)S(1)}, bf16[544,384]{1,0:T(8,128)(2,1)S(1)}, u32[]{:S(2)}, u32[]{:S(2)}) %collective-permute-start.3) | collective-permute-done | bytes 417824 | tf_op jit(solution)/shard_map/ppermute | solution.py:514
  27.5 1.6 %collective-permute-start.15 = (bf16[704,384]{1,0:T(8,128)(2,1)S(1)}, bf16[704,384]{1,0:T(8,128)(2,1)S(1)}, u32[]{:S(2)}, u32[]{:S(2)}) collective-permute-start(bf16[704,384]{1,0:T(8,128)(2,1)S(1)} %get-tuple-element.28.refs_3_), channel_id=1, source_target_pairs={{0,6},{1,7},{2,0},{3,1},{4,2},{5,3},{6,4},{7,5},{8,14},{9,15},{10,... | collective-permute-start | bytes 1622024 | tf_op jit(solution)/shard_map/ppermute | solution.py:514
  29.1 0.4 collective-permute-start.4
  29.5 0.0 collective-permute-start.5
  29.6 21.7 %collective-permute-done.5.refs_0_ = bf16[24,384]{1,0:T(8,128)(2,1)S(1)} collective-permute-done((bf16[24,384]{1,0:T(8,128)(2,1)S(1)}, bf16[24,384]{1,0:T(8,128)(2,1)S(1)}, u32[]{:S(2)}, u32[]{:S(2)}) %collective-permute-start.5) | collective-permute-done | bytes 18464 | tf_op jit(solution)/shard_map/ppermute | solution.py:514
  51.3 1.3 %collective-permute-start.8 = (bf16[24,384]{1,0:T(8,128)(2,1)S(1)}, bf16[24,384]{1,0:T(8,128)(2,1)S(1)}, u32[]{:S(2)}, u32[]{:S(2)}) collective-permute-start(bf16[24,384]{1,0:T(8,128)(2,1)S(1)} %collective-permute-done.5.refs_0_), channel_id=1, source_target_pairs={{0,24},{8,16},{16,8},{24,0},{1,25},{9,17},{17,9},{25,1},{2,26},{10... | collective-permute-start | bytes 55304 | tf_op jit(solution)/shard_map/ppermute | solution.py:521
  52.6 1.6 %collective-permute-start.7 = (bf16[24,384]{1,0:T(8,128)(2,1)S(1)}, bf16[24,384]{1,0:T(8,128)(2,1)S(1)}, u32[]{:S(2)}, u32[]{:S(2)}) collective-permute-start(bf16[24,384]{1,0:T(8,128)(2,1)S(1)} %collective-permute-done.5.refs_0_), channel_id=1, source_target_pairs={{0,16},{8,24},{16,0},{24,8},{1,17},{9,25},{17,1},{25,9},{2,18},{10... | collective-permute-start | bytes 55304 | tf_op jit(solution)/shard_map/ppermute | solution.py:521
  54.2 1.7 %collective-permute-done.8.refs_3_ = bf16[24,384]{1,0:T(8,128)(2,1)S(1)} collective-permute-done((bf16[24,384]{1,0:T(8,128)(2,1)S(1)}, bf16[24,384]{1,0:T(8,128)(2,1)S(1)}, u32[]{:S(2)}, u32[]{:S(2)}) %collective-permute-start.8) | collective-permute-done | bytes 18464 | tf_op jit(solution)/shard_map/ppermute | solution.py:521
  55.9 1.5 %collective-permute-start.6 = (bf16[24,384]{1,0:T(8,128)(2,1)S(1)}, bf16[24,384]{1,0:T(8,128)(2,1)S(1)}, u32[]{:S(2)}, u32[]{:S(2)}) collective-permute-start(bf16[24,384]{1,0:T(8,128)(2,1)S(1)} %collective-permute-done.5.refs_0_), channel_id=1, source_target_pairs={{0,8},{8,0},{16,24},{24,16},{1,9},{9,1},{17,25},{25,17},{2,10},{10... | collective-permute-start | bytes 55304 | tf_op jit(solution)/shard_map/ppermute | solution.py:521
  57.4 0.0 collective-permute-done.7.refs_2_
  57.4 2.2 %collective-permute-done.6.refs_1_ = bf16[24,384]{1,0:T(8,128)(2,1)S(1)} collective-permute-done((bf16[24,384]{1,0:T(8,128)(2,1)S(1)}, bf16[24,384]{1,0:T(8,128)(2,1)S(1)}, u32[]{:S(2)}, u32[]{:S(2)}) %collective-permute-start.6) | collective-permute-done | bytes 18464 | tf_op jit(solution)/shard_map/ppermute | solution.py:521
  59.7 0.0 collective-permute-done.9.refs_4_
  59.7 1.6 %tail.3.refs_2_ = bf16[352,384]{1,0:T(8,128)(2,1)S(1)} custom-call(bf16[24,384]{1,0:T(8,128)(2,1)S(1)} %collective-permute-done.5.refs_0_, bf16[24,384]{1,0:T(8,128)(2,1)S(1)} %collective-permute-done.6.refs_1_, bf16[24,384]{1,0:T(8,128)(2,1)S(1)} %collective-permute-done.7.refs_2_, bf16[24,384]{1,0:T(8,128)(2,1)S(1)} %collective-permute-done.8.refs_3_, ...), custom_call_target="tpu_custom_call" | custom-call | flops 138412032 | bytes 811008 | tf_op jit(solution)/shard_map/tail/pallas_call | solution.py:355
  61.3 0.0 collective-permute-done.4.refs_1_
  61.3 0.8 gram_pair.1.refs_0_
  62.1 1.4 %collective-permute-start.12 = (bf16[104,384]{1,0:T(8,128)(2,1)S(1)}, bf16[104,384]{1,0:T(8,128)(2,1)S(1)}, u32[]{:S(2)}, u32[]{:S(2)}) collective-permute-start(bf16[104,384]{1,0:T(8,128)(2,1)S(1)} %gram_pair.1.refs_0_), channel_id=1, source_target_pairs={{0,24},{8,16},{16,8},{24,0},{1,25},{9,17},{17,9},{25,1},{2,26},{10... | collective-permute-start | bytes 239624 | tf_op jit(solution)/shard_map/ppermute | solution.py:521
  63.5 1.6 %collective-permute-start.11 = (bf16[104,384]{1,0:T(8,128)(2,1)S(1)}, bf16[104,384]{1,0:T(8,128)(2,1)S(1)}, u32[]{:S(2)}, u32[]{:S(2)}) collective-permute-start(bf16[104,384]{1,0:T(8,128)(2,1)S(1)} %gram_pair.1.refs_0_), channel_id=1, source_target_pairs={{0,16},{8,24},{16,0},{24,8},{1,17},{9,25},{17,1},{25,9},{2,18},{10... | collective-permute-start | bytes 239624 | tf_op jit(solution)/shard_map/ppermute | solution.py:521
  65.2 0.5 collective-permute-start.10
  65.7 1.9 %collective-permute-done.12.refs_3_ = bf16[104,384]{1,0:T(8,128)(2,1)S(1)} collective-permute-done((bf16[104,384]{1,0:T(8,128)(2,1)S(1)}, bf16[104,384]{1,0:T(8,128)(2,1)S(1)}, u32[]{:S(2)}, u32[]{:S(2)}) %collective-permute-start.12) | collective-permute-done | bytes 79904 | tf_op jit(solution)/shard_map/ppermute | solution.py:521
  67.6 0.8 collective-permute-done.11.refs_2_
  68.4 1.2 %collective-permute-done.10.refs_1_ = bf16[104,384]{1,0:T(8,128)(2,1)S(1)} collective-permute-done((bf16[104,384]{1,0:T(8,128)(2,1)S(1)}, bf16[104,384]{1,0:T(8,128)(2,1)S(1)}, u32[]{:S(2)}, u32[]{:S(2)}) %collective-permute-start.10) | collective-permute-done | bytes 79904 | tf_op jit(solution)/shard_map/ppermute | solution.py:521
  69.6 1.6 %second.1 = (bf16[96,384]{1,0:T(8,128)(2,1)S(1)}, bf16[384,256]{1,0:T(8,128)(2,1)S(1)}) custom-call(bf16[104,384]{1,0:T(8,128)(2,1)S(1)} %gram_pair.1.refs_0_, bf16[104,384]{1,0:T(8,128)(2,1)S(1)} %collective-permute-done.10.refs_1_, bf16[104,384]{1,0:T(8,128)(2,1)S(1)} %collective-permute-done.11.refs_2_, bf16[104,384]{1,0:T(8,128)(2,1)S(1)} %collective-permute-done.12.refs_3_), custom_call_target="tpu_custom_call" | custom-call | flops 134217728 | bytes 262144 | tf_op jit(solution)/shard_map/second/pallas_call | solution.py:397
  71.2 1.7 %collective-permute-start.13 = (bf16[320,384]{1,0:T(8,128)(2,1)S(1)}, bf16[320,384]{1,0:T(8,128)(2,1)S(1)}, u32[]{:S(2)}, u32[]{:S(2)}) collective-permute-start(bf16[320,384]{1,0:T(8,128)(2,1)S(1)} %get-tuple-element.25.refs_4_), channel_id=1, source_target_pairs={{0,6},{1,7},{2,0},{3,1},{4,2},{5,3},{6,4},{7,5},{8,14},{9,15},{10,... | collective-permute-start | bytes 737288 | tf_op jit(solution)/shard_map/ppermute | solution.py:514
  72.9 0.4 collective-permute-start.14
  73.3 1.6 %tail.2.refs_2_ = bf16[352,384]{1,0:T(8,128)(2,1)S(1)} custom-call(bf16[96,384]{1,0:T(8,128)(2,1)S(1)} %get-tuple-element.19.refs_0_.s_ref, bf16[2048,384]{1,0:T(8,128)(2,1)S(1)} %copy-done.1), custom_call_target="tpu_custom_call" | custom-call | flops 138412032 | bytes 811008 | tf_op jit(solution)/shard_map/tail/pallas_call | solution.py:355
  75.0 0.8 left_half.1.refs_4_
  75.7 2.5 %collective-permute-done.14.s_ref = bf16[96,384]{1,0:T(8,128)(2,1)S(1)} collective-permute-done((bf16[96,384]{1,0:T(8,128)(2,1)S(1)}, bf16[96,384]{1,0:T(8,128)(2,1)S(1)}, u32[]{:S(2)}, u32[]{:S(2)}) %collective-permute-start.14) | collective-permute-done | bytes 73760 | tf_op jit(solution)/shard_map/ppermute | solution.py:514
  78.2 1.2 %right.1.refs_5_ = bf16[384,256]{1,0:T(8,128)(2,1)S(1)} custom-call(bf16[96,384]{1,0:T(8,128)(2,1)S(1)} %collective-permute-done.14.s_ref), custom_call_target="tpu_custom_call" | custom-call | flops 134217728 | bytes 262144 | tf_op jit(solution)/shard_map/right/pallas_call | solution.py:415
  79.4 0.0 collective-permute-done.15.refs_3_
  79.4 1.5 %final.2.refs_6_ = bf16[2048,384]{1,0:T(8,128)(2,1)} custom-call(bf16[544,384]{1,0:T(8,128)(2,1)S(1)} %get-tuple-element.17.refs_0_, bf16[128,384]{1,0:T(8,128)(2,1)S(1)} %get-tuple-element.18.refs_1_, bf16[352,384]{1,0:T(8,128)(2,1)S(1)} %tail.2.refs_2_, bf16[704,384]{1,0:T(8,128)(2,1)S(1)} %collective-permute-done.15.refs_3_, ...), custom_call_target="tpu_custom_call" | custom-call | flops 369098752 | bytes 2162688 | tf_op jit(solution)/shard_map/final/pallas_call | solution.py:496
  80.9 0.0 collective-permute-done.13.refs_3_
  81.0 1.1 %final.3 = bf16[2048,384]{1,0:T(8,128)(2,1)} custom-call(bf16[544,384]{1,0:T(8,128)(2,1)S(1)} %get-tuple-element.17.refs_0_, bf16[128,384]{1,0:T(8,128)(2,1)S(1)} %get-tuple-element.18.refs_1_, bf16[352,384]{1,0:T(8,128)(2,1)S(1)} %tail.2.refs_2_, bf16[320,384]{1,0:T(8,128)(2,1)S(1)} %collective-permute-done.13.refs_3_, ...), custom_call_target="tpu_custom_call", output_to_operand_aliasing={{}: (6, {})} | custom-call | flops 167772160 | bytes 983040 | tf_op jit(solution)/shard_map/final/pallas_call | solution.py:496
Async XLA Ops:
  0.0 1.4 %copy-start = (bf16[2048,384]{1,0:T(8,128)(2,1)S(1)}, bf16[2048,384]{1,0:T(8,128)(2,1)}, u32[]{:S(2)}) copy-start(bf16[2048,384]{1,0:T(8,128)(2,1)} %x_hbm.1) | copy-start | bytes 4718596
  1.9 15.3 %copy-start.1 = (bf16[2048,384]{1,0:T(8,128)(2,1)S(1)}, bf16[2048,384]{1,0:T(8,128)(2,1)}, u32[]{:S(2)}) copy-start(bf16[2048,384]{1,0:T(8,128)(2,1)} %x_hbm.1) | copy-start | bytes 4718596
  2.0 6.5 %collective-permute-start.2 = (bf16[104,384]{1,0:T(8,128)(2,1)S(1)}, bf16[104,384]{1,0:T(8,128)(2,1)S(1)}, u32[]{:S(2)}, u32[]{:S(2)}) collective-permute-start(bf16[104,384]{1,0:T(8,128)(2,1)S(1)} %gram.1.refs_0_), channel_id=1, source_target_pairs={{0,24},{8,16},{16,8},{24,0},{1,25},{9,17},{17,9},{25,1},{2,26},{10... | collective-permute-start | bytes 239624 | tf_op jit(solution)/shard_map/ppermute | solution.py:521
  5.9 4.4 %collective-permute-start.1 = (bf16[104,384]{1,0:T(8,128)(2,1)S(1)}, bf16[104,384]{1,0:T(8,128)(2,1)S(1)}, u32[]{:S(2)}, u32[]{:S(2)}) collective-permute-start(bf16[104,384]{1,0:T(8,128)(2,1)S(1)} %gram.1.refs_0_), channel_id=1, source_target_pairs={{0,16},{8,24},{16,0},{24,8},{1,17},{9,25},{17,1},{25,9},{2,18},{10... | collective-permute-start | bytes 239624 | tf_op jit(solution)/shard_map/ppermute | solution.py:521
  6.5 4.4 %collective-permute-start = (bf16[104,384]{1,0:T(8,128)(2,1)S(1)}, bf16[104,384]{1,0:T(8,128)(2,1)S(1)}, u32[]{:S(2)}, u32[]{:S(2)}) collective-permute-start(bf16[104,384]{1,0:T(8,128)(2,1)S(1)} %gram.1.refs_0_), channel_id=1, source_target_pairs={{0,8},{8,0},{16,24},{24,16},{1,9},{9,1},{17,25},{25,17},{2,10},{10... | collective-permute-start | bytes 239624 | tf_op jit(solution)/shard_map/ppermute | solution.py:521
  13.0 14.6 %collective-permute-start.3 = (bf16[544,384]{1,0:T(8,128)(2,1)S(1)}, bf16[544,384]{1,0:T(8,128)(2,1)S(1)}, u32[]{:S(2)}, u32[]{:S(2)}) collective-permute-start(bf16[544,384]{1,0:T(8,128)(2,1)S(1)} %get-tuple-element.17.refs_0_), channel_id=1, source_target_pairs={{0,2},{1,3},{2,4},{3,5},{4,6},{5,7},{6,0},{7,1},{8,10},{9,11},{10,... | collective-permute-start | bytes 1253384 | tf_op jit(solution)/shard_map/ppermute | solution.py:514
  15.7 44.0 %collective-permute-start.9 = (bf16[704,384]{1,0:T(8,128)(2,1)S(1)}, bf16[704,384]{1,0:T(8,128)(2,1)S(1)}, u32[]{:S(2)}, u32[]{:S(2)}) collective-permute-start(bf16[704,384]{1,0:T(8,128)(2,1)S(1)} %taken.1), channel_id=1, source_target_pairs={{0,2},{1,3},{2,4},{3,5},{4,6},{5,7},{6,0},{7,1},{8,10},{9,11},{10,... | collective-permute-start | bytes 1622024 | tf_op jit(solution)/shard_map/ppermute | solution.py:514
  27.5 51.9 %collective-permute-start.15 = (bf16[704,384]{1,0:T(8,128)(2,1)S(1)}, bf16[704,384]{1,0:T(8,128)(2,1)S(1)}, u32[]{:S(2)}, u32[]{:S(2)}) collective-permute-start(bf16[704,384]{1,0:T(8,128)(2,1)S(1)} %get-tuple-element.28.refs_3_), channel_id=1, source_target_pairs={{0,6},{1,7},{2,0},{3,1},{4,2},{5,3},{6,4},{7,5},{8,14},{9,15},{10,... | collective-permute-start | bytes 1622024 | tf_op jit(solution)/shard_map/ppermute | solution.py:514
  29.1 32.2 %collective-permute-start.4 = (bf16[128,384]{1,0:T(8,128)(2,1)S(1)}, bf16[128,384]{1,0:T(8,128)(2,1)S(1)}, u32[]{:S(2)}, u32[]{:S(2)}) collective-permute-start(bf16[128,384]{1,0:T(8,128)(2,1)S(1)} %get-tuple-element.18.refs_1_), channel_id=1, source_target_pairs={{0,2},{1,3},{2,4},{3,5},{4,6},{5,7},{6,0},{7,1},{8,10},{9,11},{10,... | collective-permute-start | bytes 294920 | tf_op jit(solution)/shard_map/ppermute | solution.py:514
  29.5 21.7 %collective-permute-start.5 = (bf16[24,384]{1,0:T(8,128)(2,1)S(1)}, bf16[24,384]{1,0:T(8,128)(2,1)S(1)}, u32[]{:S(2)}, u32[]{:S(2)}) collective-permute-start(bf16[24,384]{1,0:T(8,128)(2,1)S(1)} %get-tuple-element.22), channel_id=1, source_target_pairs={{0,2},{1,3},{2,4},{3,5},{4,6},{5,7},{6,0},{7,1},{8,10},{9,11},{10,... | collective-permute-start | bytes 55304 | tf_op jit(solution)/shard_map/ppermute | solution.py:514
  51.3 4.7 %collective-permute-start.8 = (bf16[24,384]{1,0:T(8,128)(2,1)S(1)}, bf16[24,384]{1,0:T(8,128)(2,1)S(1)}, u32[]{:S(2)}, u32[]{:S(2)}) collective-permute-start(bf16[24,384]{1,0:T(8,128)(2,1)S(1)} %collective-permute-done.5.refs_0_), channel_id=1, source_target_pairs={{0,24},{8,16},{16,8},{24,0},{1,25},{9,17},{17,9},{25,1},{2,26},{10... | collective-permute-start | bytes 55304 | tf_op jit(solution)/shard_map/ppermute | solution.py:521
  52.6 4.8 %collective-permute-start.7 = (bf16[24,384]{1,0:T(8,128)(2,1)S(1)}, bf16[24,384]{1,0:T(8,128)(2,1)S(1)}, u32[]{:S(2)}, u32[]{:S(2)}) collective-permute-start(bf16[24,384]{1,0:T(8,128)(2,1)S(1)} %collective-permute-done.5.refs_0_), channel_id=1, source_target_pairs={{0,16},{8,24},{16,0},{24,8},{1,17},{9,25},{17,1},{25,9},{2,18},{10... | collective-permute-start | bytes 55304 | tf_op jit(solution)/shard_map/ppermute | solution.py:521
  55.9 3.8 %collective-permute-start.6 = (bf16[24,384]{1,0:T(8,128)(2,1)S(1)}, bf16[24,384]{1,0:T(8,128)(2,1)S(1)}, u32[]{:S(2)}, u32[]{:S(2)}) collective-permute-start(bf16[24,384]{1,0:T(8,128)(2,1)S(1)} %collective-permute-done.5.refs_0_), channel_id=1, source_target_pairs={{0,8},{8,0},{16,24},{24,16},{1,9},{9,1},{17,25},{25,17},{2,10},{10... | collective-permute-start | bytes 55304 | tf_op jit(solution)/shard_map/ppermute | solution.py:521
  62.1 5.4 %collective-permute-start.12 = (bf16[104,384]{1,0:T(8,128)(2,1)S(1)}, bf16[104,384]{1,0:T(8,128)(2,1)S(1)}, u32[]{:S(2)}, u32[]{:S(2)}) collective-permute-start(bf16[104,384]{1,0:T(8,128)(2,1)S(1)} %gram_pair.1.refs_0_), channel_id=1, source_target_pairs={{0,24},{8,16},{16,8},{24,0},{1,25},{9,17},{17,9},{25,1},{2,26},{10... | collective-permute-start | bytes 239624 | tf_op jit(solution)/shard_map/ppermute | solution.py:521
  63.5 4.8 %collective-permute-start.11 = (bf16[104,384]{1,0:T(8,128)(2,1)S(1)}, bf16[104,384]{1,0:T(8,128)(2,1)S(1)}, u32[]{:S(2)}, u32[]{:S(2)}) collective-permute-start(bf16[104,384]{1,0:T(8,128)(2,1)S(1)} %gram_pair.1.refs_0_), channel_id=1, source_target_pairs={{0,16},{8,24},{16,0},{24,8},{1,17},{9,25},{17,1},{25,9},{2,18},{10... | collective-permute-start | bytes 239624 | tf_op jit(solution)/shard_map/ppermute | solution.py:521
  65.2 4.4 %collective-permute-start.10 = (bf16[104,384]{1,0:T(8,128)(2,1)S(1)}, bf16[104,384]{1,0:T(8,128)(2,1)S(1)}, u32[]{:S(2)}, u32[]{:S(2)}) collective-permute-start(bf16[104,384]{1,0:T(8,128)(2,1)S(1)} %gram_pair.1.refs_0_), channel_id=1, source_target_pairs={{0,8},{8,0},{16,24},{24,16},{1,9},{9,1},{17,25},{25,17},{2,10},{10... | collective-permute-start | bytes 239624 | tf_op jit(solution)/shard_map/ppermute | solution.py:521
  71.2 9.7 %collective-permute-start.13 = (bf16[320,384]{1,0:T(8,128)(2,1)S(1)}, bf16[320,384]{1,0:T(8,128)(2,1)S(1)}, u32[]{:S(2)}, u32[]{:S(2)}) collective-permute-start(bf16[320,384]{1,0:T(8,128)(2,1)S(1)} %get-tuple-element.25.refs_4_), channel_id=1, source_target_pairs={{0,6},{1,7},{2,0},{3,1},{4,2},{5,3},{6,4},{7,5},{8,14},{9,15},{10,... | collective-permute-start | bytes 737288 | tf_op jit(solution)/shard_map/ppermute | solution.py:514
  72.9 5.3 %collective-permute-start.14 = (bf16[96,384]{1,0:T(8,128)(2,1)S(1)}, bf16[96,384]{1,0:T(8,128)(2,1)S(1)}, u32[]{:S(2)}, u32[]{:S(2)}) collective-permute-start(bf16[96,384]{1,0:T(8,128)(2,1)S(1)} %get-tuple-element.27), channel_id=1, source_target_pairs={{0,6},{1,7},{2,0},{3,1},{4,2},{5,3},{6,4},{7,5},{8,14},{9,15},{10,... | collective-permute-start | bytes 221192 | tf_op jit(solution)/shard_map/ppermute | solution.py:514
